TPU v7x, 128 devices: a whole 4x4x4 slice. The times are simulated.
128 devices in a mesh: az: 16 (over z, x_hi, core), dep: 8 (over y, x_lo).
Axes of the slice: x: 4 (x_hi: 2, x_lo: 2; x = x_hi * 2 + x_lo), y: 4, z: 4, core: 2. Of those that a mesh axis runs over, the one named last changes fastest.
Arguments:
- adjoint_in: float32 [2, 2048, 4096], P(None, 'az', 'dep'), may hold values from -6 to 6
- forward_field: float32 [8, 2, 2048, 4096], P(None, None, 'az', 'dep'), may hold values from -6 to 6
- screen: float32 [2048, 4096], P('az', 'dep'), may hold values from -3.140625 to 3.140625
- bed_weight: float32 [4096], replicated, may hold values from 0.1 to 1
- labels: int32 [2048, 32], P('az'), may hold values from 0 to 31
Outputs:
- adjoint_out: float32 [2, 2048, 4096], P(None, 'az', 'dep')
- sensitivity: float32 [32], replicated
All inputs are finite; a program needn't handle non-finite values.
Results may differ from a plain program's by a relative error of at most 0.0003.
Values sent between devices are 32-bit elements; how exact they have to be, the bound alone decides.
No kernel may reach another device: no remote copies, remote signals or barrier semaphores. Data moves between devices by JAX's collectives and lax.ppermute only.
A program may use at most 128 MiB of HBM per device.

v0:
```python
import math

import jax
import jax.numpy as jnp
from jax import lax
from jax.sharding import PartitionSpec as P

GROUPS = 32


coupling = 0.15
radix_rows = 64
label_block = 128
highest = lax.Precision.HIGHEST


def padded_2(cells, sides, width):
    for axis, dim in sides:
        count = lax.axis_size(axis)
        head = lax.slice_in_dim(cells, 0, width, axis=dim)
        tail = lax.slice_in_dim(cells, cells.shape[dim] - width, cells.shape[dim], axis=dim)
        cells = jnp.concatenate(
            [
                lax.ppermute(tail, axis, [(i, (i + 1) % count) for i in range(count)]),
                cells,
                lax.ppermute(head, axis, [((i + 1) % count, i) for i in range(count)]),
            ],
            axis=dim,
        )
    return cells


def angles(left, right, modulus, sign):
    product = left[:, None] * right[None, :] % modulus
    return sign * 2.0 * math.pi * product.astype(jnp.float32) / modulus


def combine(form, real_part, imag_part, cosine, sine):
    first = jnp.einsum(form, real_part, cosine, precision=highest) - jnp.einsum(
        form, imag_part, sine, precision=highest
    )
    second = jnp.einsum(form, real_part, sine, precision=highest) + jnp.einsum(
        form, imag_part, cosine, precision=highest
    )
    return (first, second)


def transform(real_part, imag_part, sign):
    length = real_part.shape[-1]
    second_len = length // radix_rows
    leading = real_part.shape[:-1]
    shaped_re = real_part.reshape(leading + (radix_rows, second_len))
    shaped_im = imag_part.reshape(leading + (radix_rows, second_len))
    outer_idx = jnp.arange(radix_rows, dtype=jnp.int32)
    inner_idx = jnp.arange(second_len, dtype=jnp.int32)
    first_ang = angles(outer_idx, outer_idx, radix_rows, sign)
    mid_re, mid_im = combine(
        "...ab,ac->...cb", shaped_re, shaped_im, jnp.cos(first_ang), jnp.sin(first_ang)
    )
    twist = angles(outer_idx, inner_idx, length, sign)
    twist_c = jnp.cos(twist)
    twist_s = jnp.sin(twist)
    mid_re, mid_im = (mid_re * twist_c - mid_im * twist_s, mid_re * twist_s + mid_im * twist_c)
    last_ang = angles(inner_idx, inner_idx, second_len, sign)
    out_re, out_im = combine(
        "...cb,bd->...dc", mid_re, mid_im, jnp.cos(last_ang), jnp.sin(last_ang)
    )
    return (out_re.reshape(leading + (length,)), out_im.reshape(leading + (length,)))


def propagate(field):
    length = field.shape[-1]
    freq = jnp.arange(length, dtype=jnp.int32)
    freq = jnp.where(freq < length // 2, freq, freq - length).astype(jnp.float32)
    beta = 30.0 * (freq / (length // 2)) ** 2
    spec_re, spec_im = transform(field[0], field[1], -1.0)
    cos_b = jnp.cos(beta)
    sin_b = jnp.sin(beta)
    turned_re = spec_re * cos_b - spec_im * sin_b
    turned_im = spec_re * sin_b + spec_im * cos_b
    back_re, back_im = transform(turned_re, turned_im, 1.0)
    return jnp.stack([back_re, back_im]) / length


def couple(padded):
    lap_wide = padded[:, :-2] + padded[:, 2:] - 2.0 * padded[:, 1:-1]
    lap = lap_wide[:, 1:-1]
    lap_two = lap_wide[:, :-2] + lap_wide[:, 2:] - 2.0 * lap
    centre = padded[:, 2:-2]
    half = 0.5 * coupling * coupling
    new_re = centre[0] + coupling * lap[1] - half * lap_two[0]
    new_im = centre[1] - coupling * lap[0] - half * lap_two[1]
    return jnp.stack([new_re, new_im])


def group_table(marks):
    return (marks[:, :, None] == jnp.arange(GROUPS, dtype=jnp.int32)[None, None, :]).astype(
        jnp.float32
    )


def group_terms(field, stored_step, weight, onehot):
    term = (field[1] * stored_step[0] - field[0] * stored_step[1]) * weight[None, :]
    blocks = term.reshape(term.shape[0], -1, label_block).sum(-1)
    return jnp.einsum("rb,rbg->g", blocks, onehot, precision=highest)


def rotate(field, cosine, sine):
    return jnp.stack([field[0] * cosine + field[1] * sine, field[1] * cosine - field[0] * sine])


def on_device(adjoint_in, forward_field, screen, bed_weight, labels):
    steps = forward_field.shape[0]
    dep_rank = lax.axis_index("dep")
    cols_here = adjoint_in.shape[2]
    count_blocks = cols_here // label_block
    sensitivity = jnp.zeros((GROUPS,), jnp.float32)
    field = adjoint_in
    weight_cols = lax.dynamic_slice_in_dim(bed_weight, dep_rank * cols_here, cols_here, 0)
    onehot_cols = group_table(
        lax.dynamic_slice_in_dim(labels, dep_rank * count_blocks, count_blocks, 1)
    )
    cosine = jnp.cos(screen)
    sine = jnp.sin(screen)
    for step in range(steps - 1, -1, -1):
        sensitivity = sensitivity + group_terms(
            field, forward_field[step], weight_cols, onehot_cols
        )
        padded = padded_2(rotate(field, cosine, sine), (("az", 1),), 2)
        deep = lax.all_to_all(couple(padded), "dep", split_axis=1, concat_axis=2, tiled=True)
        field = lax.all_to_all(propagate(deep), "dep", split_axis=2, concat_axis=1, tiled=True)
    total = lax.psum(sensitivity, ("az", "dep"))
    return (field, total)


def solution(mesh):
    return jax.shard_map(
        on_device,
        mesh=mesh,
        in_specs=(
            P(None, "az", "dep"),
            P(None, None, "az", "dep"),
            P("az", "dep"),
            P(),
            P("az", None),
        ),
        out_specs=(P(None, "az", "dep"), P()),
        check_vma=False,
    )
```

profile of v0, /device:TPU:1, one launch (start us, length us, event | category | flops | bytes accessed | tf_op | source)
XLA Modules:
  0.0 805.0 jit_solution(5096109944816775397)
XLA Ops:
  14.0 4.4 all-to-all-start
  19.6 6.2 all-to-all-done
  47.0 4.4 copy.132
  51.4 7.2 reshape.596
  58.6 10.0 %all_to_all.243 = f32[8,1,16384]{2,1,0:T(1,128)S(1)} all-to-all(f32[8,1,16384]{2,1,0:T(1,128)S(1)} %reshape.596), channel_id=1, replica_groups=mesh['az'=16,'dep'=8] {'dep'}, dimensions={0} | all-to-all | bytes 1048576 | tf_op jit(solution)/shard_map/all_to_all | solution.py:131
  70.8 7.5 reshape.597
  78.4 5.1 copy.133
  83.7 8.8 %collective-permute-start.3 = (f32[2,2,512]{2,1,0:T(2,128)S(1)}, f32[2,2,512]{2,1,0:T(2,128)S(1)}, u32[]{:S(2)}, u32[]{:S(2)}) collective-permute-start(f32[2,2,512]{2,1,0:T(2,128)S(1)} %get-tuple-element.107), channel_id=1, source_target_pairs={{8,0},{16,8},{24,16},{32,24},{40,32},{48,40},{56,48},{64,56},{72,6... | collective-permute-start | bytes 24584 | tf_op jit(solution)/shard_map/ppermute | solution.py:26
  96.7 10.0 %all_to_all.244 = f32[2,128,512]{2,0,1:T(2,128)S(1)} all-to-all(f32[2,128,512]{2,0,1:T(2,128)S(1)} %copy.134), channel_id=1, replica_groups=mesh['az'=16,'dep'=8] {'dep'}, dimensions={1} | all-to-all | bytes 1048576 | tf_op jit(solution)/shard_map/all_to_all | solution.py:130
  129.5 4.4 copy.136
  133.8 7.2 reshape.598
  141.1 10.0 %all_to_all.245 = f32[8,1,16384]{2,1,0:T(1,128)S(1)} all-to-all(f32[8,1,16384]{2,1,0:T(1,128)S(1)} %reshape.598), channel_id=1, replica_groups=mesh['az'=16,'dep'=8] {'dep'}, dimensions={0} | all-to-all | bytes 1048576 | tf_op jit(solution)/shard_map/all_to_all | solution.py:131
  152.8 7.5 reshape.599
  160.4 5.1 copy.137
  165.7 8.7 %collective-permute-start.5 = (f32[2,2,512]{2,1,0:T(2,128)S(1)}, f32[2,2,512]{2,1,0:T(2,128)S(1)}, u32[]{:S(2)}, u32[]{:S(2)}) collective-permute-start(f32[2,2,512]{2,1,0:T(2,128)S(1)} %get-tuple-element.101), channel_id=1, source_target_pairs={{8,0},{16,8},{24,16},{32,24},{40,32},{48,40},{56,48},{64,56},{72,6... | collective-permute-start | bytes 24584 | tf_op jit(solution)/shard_map/ppermute | solution.py:26
  178.4 10.0 %all_to_all.246 = f32[2,128,512]{2,0,1:T(2,128)S(1)} all-to-all(f32[2,128,512]{2,0,1:T(2,128)S(1)} %copy.138), channel_id=1, replica_groups=mesh['az'=16,'dep'=8] {'dep'}, dimensions={1} | all-to-all | bytes 1048576 | tf_op jit(solution)/shard_map/all_to_all | solution.py:130
  206.9 2.9 fusion.10
  216.5 4.4 copy.140
  220.9 7.2 reshape.600
  228.1 10.0 %all_to_all.247 = f32[8,1,16384]{2,1,0:T(1,128)S(1)} all-to-all(f32[8,1,16384]{2,1,0:T(1,128)S(1)} %reshape.600), channel_id=1, replica_groups=mesh['az'=16,'dep'=8] {'dep'}, dimensions={0} | all-to-all | bytes 1048576 | tf_op jit(solution)/shard_map/all_to_all | solution.py:131
  239.9 7.5 reshape.601
  247.4 5.1 copy.141
  252.7 8.7 %collective-permute-start.7 = (f32[2,2,512]{2,1,0:T(2,128)S(1)}, f32[2,2,512]{2,1,0:T(2,128)S(1)}, u32[]{:S(2)}, u32[]{:S(2)}) collective-permute-start(f32[2,2,512]{2,1,0:T(2,128)S(1)} %get-tuple-element.95), channel_id=1, source_target_pairs={{8,0},{16,8},{24,16},{32,24},{40,32},{48,40},{56,48},{64,56},{72,6... | collective-permute-start | bytes 24584 | tf_op jit(solution)/shard_map/ppermute | solution.py:26
  265.4 10.0 %all_to_all.248 = f32[2,128,512]{2,0,1:T(2,128)S(1)} all-to-all(f32[2,128,512]{2,0,1:T(2,128)S(1)} %copy.142), channel_id=1, replica_groups=mesh['az'=16,'dep'=8] {'dep'}, dimensions={1} | all-to-all | bytes 1048576 | tf_op jit(solution)/shard_map/all_to_all | solution.py:130
  301.4 3.6 fusion.9
  307.2 4.4 copy.144
  311.5 7.2 reshape.602
  318.8 10.0 %all_to_all.249 = f32[8,1,16384]{2,1,0:T(1,128)S(1)} all-to-all(f32[8,1,16384]{2,1,0:T(1,128)S(1)} %reshape.602), channel_id=1, replica_groups=mesh['az'=16,'dep'=8] {'dep'}, dimensions={0} | all-to-all | bytes 1048576 | tf_op jit(solution)/shard_map/all_to_all | solution.py:131
  330.5 7.5 reshape.603
  338.1 5.1 copy.145
  343.4 8.7 %collective-permute-start.9 = (f32[2,2,512]{2,1,0:T(2,128)S(1)}, f32[2,2,512]{2,1,0:T(2,128)S(1)}, u32[]{:S(2)}, u32[]{:S(2)}) collective-permute-start(f32[2,2,512]{2,1,0:T(2,128)S(1)} %get-tuple-element.89), channel_id=1, source_target_pairs={{8,0},{16,8},{24,16},{32,24},{40,32},{48,40},{56,48},{64,56},{72,6... | collective-permute-start | bytes 24584 | tf_op jit(solution)/shard_map/ppermute | solution.py:26
  356.4 10.0 %all_to_all.250 = f32[2,128,512]{2,0,1:T(2,128)S(1)} all-to-all(f32[2,128,512]{2,0,1:T(2,128)S(1)} %copy.146), channel_id=1, replica_groups=mesh['az'=16,'dep'=8] {'dep'}, dimensions={1} | all-to-all | bytes 1048576 | tf_op jit(solution)/shard_map/all_to_all | solution.py:130
  392.4 3.6 fusion.7
  398.2 4.4 copy.148
  402.5 7.2 reshape.604
  409.8 10.0 %all_to_all.251 = f32[8,1,16384]{2,1,0:T(1,128)S(1)} all-to-all(f32[8,1,16384]{2,1,0:T(1,128)S(1)} %reshape.604), channel_id=1, replica_groups=mesh['az'=16,'dep'=8] {'dep'}, dimensions={0} | all-to-all | bytes 1048576 | tf_op jit(solution)/shard_map/all_to_all | solution.py:131
  421.5 7.5 reshape.605
  429.1 5.1 copy.149
  434.4 8.6 %collective-permute-start.11 = (f32[2,2,512]{2,1,0:T(2,128)S(1)}, f32[2,2,512]{2,1,0:T(2,128)S(1)}, u32[]{:S(2)}, u32[]{:S(2)}) collective-permute-start(f32[2,2,512]{2,1,0:T(2,128)S(1)} %get-tuple-element.83), channel_id=1, source_target_pairs={{8,0},{16,8},{24,16},{32,24},{40,32},{48,40},{56,48},{64,56},{72,6... | collective-permute-start | bytes 24584 | tf_op jit(solution)/shard_map/ppermute | solution.py:26
  447.4 10.0 %all_to_all.252 = f32[2,128,512]{2,0,1:T(2,128)S(1)} all-to-all(f32[2,128,512]{2,0,1:T(2,128)S(1)} %copy.150), channel_id=1, replica_groups=mesh['az'=16,'dep'=8] {'dep'}, dimensions={1} | all-to-all | bytes 1048576 | tf_op jit(solution)/shard_map/all_to_all | solution.py:130
  483.5 3.6 fusion.5
  489.2 4.4 copy.152
  493.6 7.2 reshape.606
  500.8 10.0 %all_to_all.253 = f32[8,1,16384]{2,1,0:T(1,128)S(1)} all-to-all(f32[8,1,16384]{2,1,0:T(1,128)S(1)} %reshape.606), channel_id=1, replica_groups=mesh['az'=16,'dep'=8] {'dep'}, dimensions={0} | all-to-all | bytes 1048576 | tf_op jit(solution)/shard_map/all_to_all | solution.py:131
  512.6 7.5 reshape.607
  520.1 5.1 copy.153
  525.5 8.7 %collective-permute-start.13 = (f32[2,2,512]{2,1,0:T(2,128)S(1)}, f32[2,2,512]{2,1,0:T(2,128)S(1)}, u32[]{:S(2)}, u32[]{:S(2)}) collective-permute-start(f32[2,2,512]{2,1,0:T(2,128)S(1)} %get-tuple-element.77), channel_id=1, source_target_pairs={{8,0},{16,8},{24,16},{32,24},{40,32},{48,40},{56,48},{64,56},{72,6... | collective-permute-start | bytes 24584 | tf_op jit(solution)/shard_map/ppermute | solution.py:26
  538.5 10.0 %all_to_all.254 = f32[2,128,512]{2,0,1:T(2,128)S(1)} all-to-all(f32[2,128,512]{2,0,1:T(2,128)S(1)} %copy.154), channel_id=1, replica_groups=mesh['az'=16,'dep'=8] {'dep'}, dimensions={1} | all-to-all | bytes 1048576 | tf_op jit(solution)/shard_map/all_to_all | solution.py:130
  574.6 3.6 fusion.3
  580.3 4.4 copy.156
  584.7 7.9 reshape.608
  592.6 3.5 all-to-all-start.13
  597.6 4.2 fusion.951
  605.3 7.5 reshape.609
  612.9 5.1 copy.157
  618.2 8.5 %collective-permute-start.15 = (f32[2,2,512]{2,1,0:T(2,128)S(1)}, f32[2,2,512]{2,1,0:T(2,128)S(1)}, u32[]{:S(2)}, u32[]{:S(2)}) collective-permute-start(f32[2,2,512]{2,1,0:T(2,128)S(1)} %get-tuple-element.71), channel_id=1, source_target_pairs={{8,0},{16,8},{24,16},{32,24},{40,32},{48,40},{56,48},{64,56},{72,6... | collective-permute-start | bytes 24584 | tf_op jit(solution)/shard_map/ppermute | solution.py:26
  667.7 3.8 all-to-all-start.14
  671.5 3.4 multiply_reduce_fusion.6
  700.2 4.4 copy.160
  704.5 7.9 reshape.610
  712.4 5.1 all-to-all-start.15
  719.1 70.0 %psum.7 = f32[32]{0:T(128)} all-reduce(f32[32]{0:T(128)S(1)} %add_add_fusion), channel_id=1, replica_groups=mesh['az'=16,'dep'=8] {'az','dep'}, use_global_device_ids=true, to_apply=%region_8.9 | all-reduce | flops 32 | bytes 256 | tf_op jit(solution)/shard_map/psum | solution.py:132
  790.9 7.6 reshape.611
  798.5 6.3 copy.161
  (380 shorter events, 308.4 us)
Async XLA Ops:
  0.6 596.3 %copy-start = (f32[4096]{0:T(1024)S(1)}, f32[4096]{0:T(1024)}, u32[]{:S(2)}) copy-start(f32[4096]{0:T(1024)} %param.8) | copy-start | bytes 49156
  3.7 5.5 collective-permute-start.1
  5.2 6.7 collective-permute-start
  14.0 11.8 %all-to-all-start = ((f32[2,128,512]{2,0,1:T(2,128)}), f32[2,128,512]{2,0,1:T(2,128)S(1)}, u32[]{:S(2)}, u32[]{:S(2)}) async-start(f32[2,128,512]{2,0,1:T(2,128)} %pad_maximum_fusion.24), calls=%async_computation | async-start | bytes 1048576 | tf_op jit(solution)/shard_map/all_to_all | solution.py:130
  83.7 9.6 %collective-permute-start.3 = (f32[2,2,512]{2,1,0:T(2,128)S(1)}, f32[2,2,512]{2,1,0:T(2,128)S(1)}, u32[]{:S(2)}, u32[]{:S(2)}) collective-permute-start(f32[2,2,512]{2,1,0:T(2,128)S(1)} %get-tuple-element.107), channel_id=1, source_target_pairs={{8,0},{16,8},{24,16},{32,24},{40,32},{48,40},{56,48},{64,56},{72,6... | collective-permute-start | bytes 24584 | tf_op jit(solution)/shard_map/ppermute | solution.py:26
  92.5 3.3 collective-permute-start.2
  165.7 9.5 %collective-permute-start.5 = (f32[2,2,512]{2,1,0:T(2,128)S(1)}, f32[2,2,512]{2,1,0:T(2,128)S(1)}, u32[]{:S(2)}, u32[]{:S(2)}) collective-permute-start(f32[2,2,512]{2,1,0:T(2,128)S(1)} %get-tuple-element.101), channel_id=1, source_target_pairs={{8,0},{16,8},{24,16},{32,24},{40,32},{48,40},{56,48},{64,56},{72,6... | collective-permute-start | bytes 24584 | tf_op jit(solution)/shard_map/ppermute | solution.py:26
  174.3 3.2 collective-permute-start.4
  252.7 9.5 %collective-permute-start.7 = (f32[2,2,512]{2,1,0:T(2,128)S(1)}, f32[2,2,512]{2,1,0:T(2,128)S(1)}, u32[]{:S(2)}, u32[]{:S(2)}) collective-permute-start(f32[2,2,512]{2,1,0:T(2,128)S(1)} %get-tuple-element.95), channel_id=1, source_target_pairs={{8,0},{16,8},{24,16},{32,24},{40,32},{48,40},{56,48},{64,56},{72,6... | collective-permute-start | bytes 24584 | tf_op jit(solution)/shard_map/ppermute | solution.py:26
  261.4 3.1 collective-permute-start.6
  343.3 9.6 %copy-start.1 = (f32[1,8,16,512]{3,2,1,0:T(8,128)}, f32[1,8,16,512]{3,2,1,0:T(8,128)S(1)}, u32[]{:S(2)}) copy-start(f32[1,8,16,512]{3,2,1,0:T(8,128)S(1)} %get-tuple-element.91) | copy-start | bytes 786436
  343.3 9.6 %copy-start.3 = (f32[1,8,16,512]{3,2,1,0:T(8,128)}, f32[1,8,16,512]{3,2,1,0:T(8,128)S(1)}, u32[]{:S(2)}) copy-start(f32[1,8,16,512]{3,2,1,0:T(8,128)S(1)} %get-tuple-element.90) | copy-start | bytes 786436
  343.4 9.5 %collective-permute-start.9 = (f32[2,2,512]{2,1,0:T(2,128)S(1)}, f32[2,2,512]{2,1,0:T(2,128)S(1)}, u32[]{:S(2)}, u32[]{:S(2)}) collective-permute-start(f32[2,2,512]{2,1,0:T(2,128)S(1)} %get-tuple-element.89), channel_id=1, source_target_pairs={{8,0},{16,8},{24,16},{32,24},{40,32},{48,40},{56,48},{64,56},{72,6... | collective-permute-start | bytes 24584 | tf_op jit(solution)/shard_map/ppermute | solution.py:26
  352.1 3.4 collective-permute-start.8
  434.3 9.6 %copy-start.5 = (f32[1,8,16,512]{3,2,1,0:T(8,128)}, f32[1,8,16,512]{3,2,1,0:T(8,128)S(1)}, u32[]{:S(2)}) copy-start(f32[1,8,16,512]{3,2,1,0:T(8,128)S(1)} %get-tuple-element.85) | copy-start | bytes 786436
  434.3 9.6 %copy-start.7 = (f32[1,8,16,512]{3,2,1,0:T(8,128)}, f32[1,8,16,512]{3,2,1,0:T(8,128)S(1)}, u32[]{:S(2)}) copy-start(f32[1,8,16,512]{3,2,1,0:T(8,128)S(1)} %get-tuple-element.84) | copy-start | bytes 786436
  434.4 9.4 %collective-permute-start.11 = (f32[2,2,512]{2,1,0:T(2,128)S(1)}, f32[2,2,512]{2,1,0:T(2,128)S(1)}, u32[]{:S(2)}, u32[]{:S(2)}) collective-permute-start(f32[2,2,512]{2,1,0:T(2,128)S(1)} %get-tuple-element.83), channel_id=1, source_target_pairs={{8,0},{16,8},{24,16},{32,24},{40,32},{48,40},{56,48},{64,56},{72,6... | collective-permute-start | bytes 24584 | tf_op jit(solution)/shard_map/ppermute | solution.py:26
  443.0 3.5 collective-permute-start.10
  525.3 9.6 %copy-start.9 = (f32[1,8,16,512]{3,2,1,0:T(8,128)}, f32[1,8,16,512]{3,2,1,0:T(8,128)S(1)}, u32[]{:S(2)}) copy-start(f32[1,8,16,512]{3,2,1,0:T(8,128)S(1)} %get-tuple-element.79) | copy-start | bytes 786436
  525.3 9.6 %copy-start.11 = (f32[1,8,16,512]{3,2,1,0:T(8,128)}, f32[1,8,16,512]{3,2,1,0:T(8,128)S(1)}, u32[]{:S(2)}) copy-start(f32[1,8,16,512]{3,2,1,0:T(8,128)S(1)} %get-tuple-element.78) | copy-start | bytes 786436
  525.5 9.5 %collective-permute-start.13 = (f32[2,2,512]{2,1,0:T(2,128)S(1)}, f32[2,2,512]{2,1,0:T(2,128)S(1)}, u32[]{:S(2)}, u32[]{:S(2)}) collective-permute-start(f32[2,2,512]{2,1,0:T(2,128)S(1)} %get-tuple-element.77), channel_id=1, source_target_pairs={{8,0},{16,8},{24,16},{32,24},{40,32},{48,40},{56,48},{64,56},{72,6... | collective-permute-start | bytes 24584 | tf_op jit(solution)/shard_map/ppermute | solution.py:26
  534.1 3.5 collective-permute-start.12
  580.3 15.8 %copy-start.13 = (f32[2,128,512]{2,1,0:T(8,128)S(1)}, f32[2,128,512]{2,1,0:T(8,128)}, u32[]{:S(2)}) copy-start(f32[2,128,512]{2,1,0:T(8,128)} %param.5) | copy-start | bytes 1572868
  592.6 11.0 %all-to-all-start.13 = ((f32[8,1,16384]{2,1,0:T(1,128)}), f32[8,1,16384]{2,1,0:T(1,128)S(1)}, u32[]{:S(2)}, u32[]{:S(2)}) async-start(f32[8,1,16384]{2,1,0:T(1,128)} %reshape.608), calls=%async_computation.13 | async-start | bytes 1048576 | tf_op jit(solution)/shard_map/all_to_all | solution.py:131
  618.2 47.7 %collective-permute-start.15 = (f32[2,2,512]{2,1,0:T(2,128)S(1)}, f32[2,2,512]{2,1,0:T(2,128)S(1)}, u32[]{:S(2)}, u32[]{:S(2)}) collective-permute-start(f32[2,2,512]{2,1,0:T(2,128)S(1)} %get-tuple-element.71), channel_id=1, source_target_pairs={{8,0},{16,8},{24,16},{32,24},{40,32},{48,40},{56,48},{64,56},{72,6... | collective-permute-start | bytes 24584 | tf_op jit(solution)/shard_map/ppermute | solution.py:26
  626.7 39.2 %collective-permute-start.14 = (f32[2,2,512]{2,1,0:T(2,128)S(1)}, f32[2,2,512]{2,1,0:T(2,128)S(1)}, u32[]{:S(2)}, u32[]{:S(2)}) collective-permute-start(f32[2,2,512]{2,1,0:T(2,128)S(1)} %get-tuple-element.70), channel_id=1, source_target_pairs={{0,8},{8,16},{16,24},{24,32},{32,40},{40,48},{48,56},{56,64},{64,7... | collective-permute-start | bytes 24584 | tf_op jit(solution)/shard_map/ppermute | solution.py:24
  642.1 22.3 %copy-start.4 = (f32[1,8,16,512]{3,2,1,0:T(8,128)S(1)}, f32[1,8,16,512]{3,2,1,0:T(8,128)}, u32[]{:S(2)}) copy-start(f32[1,8,16,512]{3,2,1,0:T(8,128)} %copy-done.3) | copy-start | bytes 786436
  643.8 21.3 %copy-start.2 = (f32[1,8,16,512]{3,2,1,0:T(8,128)S(1)}, f32[1,8,16,512]{3,2,1,0:T(8,128)}, u32[]{:S(2)}) copy-start(f32[1,8,16,512]{3,2,1,0:T(8,128)} %copy-done.1) | copy-start | bytes 786436
  666.4 8.5 %copy-start.8 = (f32[1,8,16,512]{3,2,1,0:T(8,128)S(1)}, f32[1,8,16,512]{3,2,1,0:T(8,128)}, u32[]{:S(2)}) copy-start(f32[1,8,16,512]{3,2,1,0:T(8,128)} %copy-done.7) | copy-start | bytes 786436
  666.4 9.3 %copy-start.6 = (f32[1,8,16,512]{3,2,1,0:T(8,128)S(1)}, f32[1,8,16,512]{3,2,1,0:T(8,128)}, u32[]{:S(2)}) copy-start(f32[1,8,16,512]{3,2,1,0:T(8,128)} %copy-done.5) | copy-start | bytes 786436
  666.4 9.4 %copy-start.12 = (f32[1,8,16,512]{3,2,1,0:T(8,128)S(1)}, f32[1,8,16,512]{3,2,1,0:T(8,128)}, u32[]{:S(2)}) copy-start(f32[1,8,16,512]{3,2,1,0:T(8,128)} %copy-done.11) | copy-start | bytes 786436
  666.5 9.4 %copy-start.10 = (f32[1,8,16,512]{3,2,1,0:T(8,128)S(1)}, f32[1,8,16,512]{3,2,1,0:T(8,128)}, u32[]{:S(2)}) copy-start(f32[1,8,16,512]{3,2,1,0:T(8,128)} %copy-done.9) | copy-start | bytes 786436
  667.7 8.5 %copy-start.14 = (f32[128,4,128]{2,1,0:T(4,128)S(1)}, f32[128,4,128]{2,1,0:T(4,128)}, u32[]{:S(2)}) copy-start(f32[128,4,128]{2,1,0:T(4,128)} %squeeze.218) | copy-start | bytes 786436
  667.7 8.6 %copy-start.15 = (f32[128,4,128]{2,1,0:T(4,128)S(1)}, f32[128,4,128]{2,1,0:T(4,128)}, u32[]{:S(2)}) copy-start(f32[128,4,128]{2,1,0:T(4,128)} %squeeze.219) | copy-start | bytes 786436
  667.7 8.6 %copy-start.16 = (f32[128,4,128]{2,1,0:T(4,128)S(1)}, f32[128,4,128]{2,1,0:T(4,128)}, u32[]{:S(2)}) copy-start(f32[128,4,128]{2,1,0:T(4,128)} %squeeze.216) | copy-start | bytes 786436
  667.7 8.6 %copy-start.17 = (f32[128,4,128]{2,1,0:T(4,128)S(1)}, f32[128,4,128]{2,1,0:T(4,128)}, u32[]{:S(2)}) copy-start(f32[128,4,128]{2,1,0:T(4,128)} %squeeze.217) | copy-start | bytes 786436
  667.7 11.4 %all-to-all-start.14 = ((f32[2,128,512]{2,0,1:T(2,128)}), f32[2,128,512]{2,0,1:T(2,128)S(1)}, u32[]{:S(2)}, u32[]{:S(2)}) async-start(f32[2,128,512]{2,0,1:T(2,128)} %copy.158), calls=%async_computation.14 | async-start | bytes 1048576 | tf_op jit(solution)/shard_map/all_to_all | solution.py:130
  700.1 17.3 %copy-start.18 = (f32[128,4]{1,0:T(8,128)S(1)}, f32[128,4]{1,0:T(8,128)}, u32[]{:S(2)}) copy-start(f32[128,4]{1,0:T(8,128)} %get-tuple-element.13) | copy-start | bytes 6148
  700.1 17.3 %copy-start.19 = (f32[128,4]{1,0:T(8,128)S(1)}, f32[128,4]{1,0:T(8,128)}, u32[]{:S(2)}) copy-start(f32[128,4]{1,0:T(8,128)} %get-tuple-element.14) | copy-start | bytes 6148
  700.1 17.3 %copy-start.20 = (f32[128,4]{1,0:T(8,128)S(1)}, f32[128,4]{1,0:T(8,128)}, u32[]{:S(2)}) copy-start(f32[128,4]{1,0:T(8,128)} %get-tuple-element.15) | copy-start | bytes 6148
  700.1 17.3 %copy-start.21 = (f32[128,4]{1,0:T(8,128)S(1)}, f32[128,4]{1,0:T(8,128)}, u32[]{:S(2)}) copy-start(f32[128,4]{1,0:T(8,128)} %get-tuple-element.16) | copy-start | bytes 6148
  700.1 17.3 %copy-start.22 = (f32[128,4]{1,0:T(8,128)S(1)}, f32[128,4]{1,0:T(8,128)}, u32[]{:S(2)}) copy-start(f32[128,4]{1,0:T(8,128)} %get-tuple-element.17) | copy-start | bytes 6148
  700.2 17.3 %copy-start.23 = (s32[128,4]{1,0:T(8,128)S(1)}, s32[128,4]{1,0:T(8,128)}, u32[]{:S(2)}) copy-start(s32[128,4]{1,0:T(8,128)} %copy.162) | copy-start | bytes 6148
  712.4 76.7 %all-to-all-start.15 = ((f32[8,1,16384]{2,1,0:T(1,128)}), f32[8,1,16384]{2,1,0:T(1,128)S(1)}, u32[]{:S(2)}, u32[]{:S(2)}) async-start(f32[8,1,16384]{2,1,0:T(1,128)} %reshape.610), calls=%async_computation.15 | async-start | bytes 1048576 | tf_op jit(solution)/shard_map/all_to_all | solution.py:131
where the time goes:
time: 812 us; the launch traced here: 805 us
  local copies, waits for them, and re-layouts  281 us (35%)
  blocking collectives  189 us (23%)
  matrix products  183 us (23%)
  starting transfers between devices  82 us (10%)
  other arithmetic  36 us (4%)
  waiting for transfers between devices  31.1 us (4%)
    unnamed x64, local copies, waits for them, and re-layouts  120 us
    psum x1, blocking collectives, on_device(): total = lax.psum(sensitivity, ('az', 'dep'))  70 us
    ppermute x8, starting transfers between devices, padded_2(): lax.ppermute(head, axis, [((i + 1) % count, i) for i in range(count)])  62 us
    all_to_all x6, blocking collectives, on_device(): lax.all_to_all(propagate(deep), 'dep', split_axis=2, concat_axis=1, tiled...  59.7 us
    all_to_all x6, blocking collectives, on_device(): lax.all_to_all(couple(padded), 'dep', split_axis=1, concat_axis=2, tiled=...  59.7 us
    dot_general x32, matrix products, combine(): jnp.einsum(form, imag_part, cosine, precision=highest)  50 us
    dot_general x32, matrix products, combine(): jnp.einsum(form, imag_part, sine, precision=highest)  47.5 us
    dot_general x32, matrix products, combine(): jnp.einsum(form, real_part, cosine, precision=highest)  43 us
  transfers between devices with their start and end apart: 20, of which 16 were waited for; matrix products, arithmetic and copies ran while one was open for 7% of the time, Pallas kernels for 0%

commit v1 on v0

v1 whole, which is shorter than its diff:
```python
import math

import jax
import jax.numpy as jnp
import ml_dtypes
import numpy as np
from jax import lax
from jax.experimental import pallas as pl
from jax.experimental.pallas import tpu as pltpu
from jax.sharding import PartitionSpec as P

GROUPS = 32
COUPLING = 0.15
LABEL_BLOCK = 128
LANES = 128
ROW_PAD = 8


def split_table(table):
    high = table.astype(ml_dtypes.bfloat16)
    low = (table - high.astype(np.float64)).astype(ml_dtypes.bfloat16)
    return np.stack([high, low])


def transform_tables(depths):
    blocks = depths // LANES
    lane = np.arange(LANES)
    turn = 2.0 * np.pi * (np.outer(lane, lane) % LANES) / LANES
    cosine, sine = np.cos(turn), np.sin(turn)
    ahead = np.block([[cosine, -sine], [sine, cosine]])
    back = np.block([[cosine, sine], [-sine, cosine]])
    outer = np.arange(blocks)
    twist = 2.0 * np.pi * np.outer(outer, lane) / depths
    freq = outer[:, None] + blocks * lane[None, :]
    freq = np.where(freq < depths // 2, freq, freq - depths)
    beta = 30.0 * (freq / (depths // 2)) ** 2
    tables = np.stack([np.cos(twist), -np.sin(twist), np.cos(beta) / depths, np.sin(beta) / depths])
    return (
        split_table(ahead),
        split_table(back),
        tables[:, :, None, :].astype(np.float32),
    )


def times(value, factor):
    return (value[0] * factor[0] - value[1] * factor[1], value[0] * factor[1] + value[1] * factor[0])


def times_fixed(value, angle):
    c, s = math.cos(angle), math.sin(angle)
    if abs(s) < 1e-12:
        return value if c > 0 else (-value[0], -value[1])
    if abs(c) < 1e-12:
        return (-value[1], value[0]) if s > 0 else (value[1], -value[0])
    if abs(abs(c) - abs(s)) < 1e-12:
        root = math.sqrt(0.5)
        re = value[0] * math.copysign(1, c) - value[1] * math.copysign(1, s)
        im = value[0] * math.copysign(1, s) + value[1] * math.copysign(1, c)
        return (re * root, im * root)
    return (value[0] * c - value[1] * s, value[0] * s + value[1] * c)


def plus(a, b):
    return (a[0] + b[0], a[1] + b[1])


def minus(a, b):
    return (a[0] - b[0], a[1] - b[1])


def small_dft(values, sign):
    count = len(values)
    if count == 1:
        return values
    even = small_dft(values[0::2], sign)
    odd = small_dft(values[1::2], sign)
    odd = [times_fixed(v, sign * 2.0 * math.pi * k / count) for k, v in enumerate(odd)]
    return [plus(e, o) for e, o in zip(even, odd)] + [minus(e, o) for e, o in zip(even, odd)]


def sine_cosine(angle):
    half = 0.5 * angle
    square = half * half
    s = jnp.full_like(square, 1.0 / math.factorial(13))
    for order in (11, 9, 7, 5, 3, 1):
        s = s * square + (-1.0) ** (order // 2) / math.factorial(order)
    s = s * half
    c = jnp.full_like(square, 1.0 / math.factorial(12))
    for order in (10, 8, 6, 4, 2, 0):
        c = c * square + (-1.0) ** (order // 2) / math.factorial(order)
    return 2.0 * s * c, 1.0 - 2.0 * s * s


def steps_kernel(steps, halo, window, ahead, back, tables, past, out, scr, angle_c, angle_s, mid, high, low):
    outer, inner = mid.shape[1], mid.shape[2]
    blocks = outer * inner
    rows = window.shape[2]
    own = rows - 2 * halo
    root_angle = 2.0 * math.pi / blocks
    half = 0.5 * COUPLING * COUPLING

    scr[:, :, :, 0:ROW_PAD] = jnp.zeros((2, outer, inner, ROW_PAD, LANES), jnp.float32)
    scr[:, :, :, ROW_PAD + rows :] = jnp.zeros((2, outer, inner, ROW_PAD, LANES), jnp.float32)

    def turn_screen(value, p, q, base):
        c = angle_c[p, q, base : base + 8]
        s = angle_s[p, q, base : base + 8]
        scr[0, p, q, base + ROW_PAD : base + ROW_PAD + 8] = value[0] * c + value[1] * s
        scr[1, p, q, base + ROW_PAD : base + ROW_PAD + 8] = value[1] * c - value[0] * s

    def start(p, carry):
        for q in range(inner):
            lanes = slice(q * LANES, (q + 1) * LANES)
            for base in range(0, rows, 8):
                at = slice(base, base + 8)
                s, c = sine_cosine(window[p, 2, at, lanes])
                angle_c[p, q, at] = c
                angle_s[p, q, at] = s
                turn_screen((window[p, 0, at, lanes], window[p, 1, at, lanes]), p, q, base)
        return carry

    lax.fori_loop(0, outer, start, 0)

    def couple(p, q, base):
        def at(part, shift):
            begin = base + ROW_PAD + shift
            return scr[part, p, q, begin : begin + 8]

        centre = [at(part, 0) for part in range(2)]
        near = [at(part, 1) + at(part, -1) for part in range(2)]
        far = [at(part, 2) + at(part, -2) for part in range(2)]
        lap = [near[part] - 2.0 * centre[part] for part in range(2)]
        lap_two = [far[part] - 4.0 * near[part] + 6.0 * centre[part] for part in range(2)]
        return (
            centre[0] + COUPLING * lap[1] - half * lap_two[0],
            centre[1] - COUPLING * lap[0] - half * lap_two[1],
        )

    def step(index, first, count, last):
        for q in range(inner):
            for base in range(first, first + count, 8):
                turned = small_dft([couple(p, q, base) for p in range(outer)], -1.0)
                for kp in range(outer):
                    value = times_fixed(turned[kp], -root_angle * q * kp)
                    mid[0, kp, q, base : base + 8] = value[0]
                    mid[1, kp, q, base : base + 8] = value[1]
        for kp in range(outer):
            for base in range(first, first + count, 16):
                at = slice(base, base + 16)
                turned = small_dft([(mid[0, kp, q, at], mid[1, kp, q, at]) for q in range(inner)], -1.0)
                for kq in range(inner):
                    k1 = kp + outer * kq
                    value = times(turned[kq], (tables[0, k1], tables[1, k1]))
                    for part in range(2):
                        lanes = slice(part * LANES, (part + 1) * LANES)
                        head = value[part].astype(jnp.bfloat16)
                        packed = slice(base - first, base - first + 16)
                        high[kp, kq, packed, lanes] = head
                        low[kp, kq, packed, lanes] = (value[part] - head.astype(jnp.float32)).astype(jnp.bfloat16)
        shape = (inner * count, 2 * LANES)
        rng = slice(first, first + count)

        def product(head, tail, table):
            def dot(a, b):
                return lax.dot_general(a, b, (((1,), (0,)), ((), ())), preferred_element_type=jnp.float32)

            return dot(head, table[0]) + dot(tail, table[0]) + dot(head, table[1])

        for kp in range(outer):
            head = high[kp, :, :count].reshape(shape)
            tail = low[kp, :, :count].reshape(shape)
            spec = product(head, tail, ahead)
            spec_re = spec[:, :LANES].reshape(inner, count, LANES)
            spec_im = spec[:, LANES:].reshape(inner, count, LANES)
            phase_c = jnp.stack([tables[2, kp + outer * kq] for kq in range(inner)])
            phase_s = jnp.stack([tables[3, kp + outer * kq] for kq in range(inner)])
            spec_re, spec_im = times((spec_re, spec_im), (phase_c, phase_s))
            spec = jnp.concatenate([spec_re.reshape(shape[0], LANES), spec_im.reshape(shape[0], LANES)], axis=1)
            head = spec.astype(jnp.bfloat16)
            tail = (spec - head.astype(jnp.float32)).astype(jnp.bfloat16)
            spec = product(head, tail, back)
            mid[0, kp, :, rng] = spec[:, :LANES].reshape(inner, count, LANES)
            mid[1, kp, :, rng] = spec[:, LANES:].reshape(inner, count, LANES)
        for kp in range(outer):
            for base in range(first, first + count, 8):
                at = slice(base, base + 8)
                values = []
                for kq in range(inner):
                    k1 = kp + outer * kq
                    values.append(times((mid[0, kp, kq, at], mid[1, kp, kq, at]), (tables[0, k1], -tables[1, k1])))
                turned = small_dft(values, 1.0)
                for q in range(inner):
                    value = times_fixed(turned[q], root_angle * q * kp)
                    mid[0, kp, q, at] = value[0]
                    mid[1, kp, q, at] = value[1]
        for q in range(inner):
            lanes = slice(q * LANES, (q + 1) * LANES)
            for base in range(first, first + count, 8):
                at = slice(base, base + 8)
                turned = small_dft([(mid[0, kp, q, at], mid[1, kp, q, at]) for kp in range(outer)], 1.0)
                for p in range(outer):
                    if halo <= base < halo + own:
                        centre = slice(base - halo, base - halo + 8)
                        for part in range(2):
                            if last:
                                out[p, part, centre, lanes] = turned[p][part]
                            else:
                                past[p, index, part, centre, lanes] = turned[p][part]
                    if not last:
                        turn_screen(turned[p], p, q, base)

    spans = []
    for index in range(steps):
        first = 2 * (index + 1) // 8 * 8
        spans.append((first, rows - 2 * first))
    index = 0
    while index < steps:
        stop = index
        while stop < steps - 1 and spans[stop] == spans[index]:
            stop += 1
        if index == steps - 1:
            step(index, *spans[index], True)
            break
        if stop == index:
            stop = index + 1

        def run(at, carry, span=spans[index]):
            step(at, *span, False)
            return carry

        lax.fori_loop(index, stop, run, 0)
        index = stop


def run_steps(window, steps, halo):
    sources, _, rows, cols = window.shape
    inner = cols // LANES
    ahead, back, tables = transform_tables(sources * cols)
    own = rows - 2 * halo
    vmem = pl.BlockSpec(memory_space=pltpu.VMEM)
    field = (sources, inner)
    return pl.pallas_call(
        lambda *refs: steps_kernel(steps, halo, *refs),
        out_shape=(
            jax.ShapeDtypeStruct((sources, steps - 1, 2, own, cols), jnp.float32),
            jax.ShapeDtypeStruct((sources, 2, own, cols), jnp.float32),
        ),
        in_specs=[vmem] * 4,
        out_specs=(vmem, vmem),
        scratch_shapes=[
            pltpu.VMEM((2,) + field + (rows + 2 * ROW_PAD, LANES), jnp.float32),
            pltpu.VMEM(field + (rows, LANES), jnp.float32),
            pltpu.VMEM(field + (rows, LANES), jnp.float32),
            pltpu.VMEM((2,) + field + (rows, LANES), jnp.float32),
            pltpu.VMEM(field + (rows, 2 * LANES), jnp.bfloat16),
            pltpu.VMEM(field + (rows, 2 * LANES), jnp.bfloat16),
        ],
        compiler_params=pltpu.CompilerParams(vmem_limit_bytes=40 * 1024 * 1024),
        name="steps",
    )(window, jnp.asarray(ahead), jnp.asarray(back), jnp.asarray(tables))


def group_sums(blocks, marks):
    hit = marks[:, :, None] == jnp.arange(GROUPS, dtype=jnp.int32)
    return jnp.sum(jnp.where(hit, blocks[:, :, None], 0.0), axis=(0, 1))


def block_sums(term):
    return term.reshape(term.shape[:-1] + (-1, LABEL_BLOCK)).sum(-1)


def on_device(adjoint_in, forward_field, screen, bed_weight, labels):
    steps = forward_field.shape[0]
    sectors = lax.axis_size("az")
    ranges = lax.axis_size("dep")
    rank = lax.axis_index("dep")
    rows_here, cols_here = screen.shape
    own = rows_here // ranges
    halo = 2 * steps
    blocks_here = cols_here // LABEL_BLOCK

    stacked = jnp.concatenate([adjoint_in, screen[None]])
    ahead = [(i, (i + 1) % sectors) for i in range(sectors)]
    behind = [((i + 1) % sectors, i) for i in range(sectors)]
    above = lax.ppermute(stacked[:, rows_here - halo :], "az", ahead)
    below = lax.ppermute(stacked[:, :halo], "az", behind)
    wide = jnp.concatenate([above, stacked, below], axis=1)
    windows = jnp.stack([wide[:, d * own : (d + 1) * own + 2 * halo] for d in range(ranges)])
    window = lax.all_to_all(windows, "dep", 0, 0)

    stored = forward_field[: steps - 1].reshape(steps - 1, 2, ranges, own, cols_here)
    stored = lax.all_to_all(jnp.transpose(stored, (2, 0, 1, 3, 4)), "dep", 0, 0)

    past, final = run_steps(window, steps, halo)
    field = lax.all_to_all(final, "dep", 0, 0)
    field = jnp.transpose(field, (1, 0, 2, 3)).reshape(2, rows_here, cols_here)

    stored = stored[:, ::-1]
    term = jnp.sum(past[:, :, 1] * stored[:, :, 0] - past[:, :, 0] * stored[:, :, 1], axis=1)
    term = term * bed_weight.reshape(ranges, 1, cols_here)
    marks = lax.dynamic_slice_in_dim(labels, rank * own, own, 0)
    blocks = block_sums(term)
    marks = jnp.transpose(marks.reshape(own, ranges, blocks_here), (1, 0, 2))
    sums = group_sums(blocks.reshape(ranges * own, blocks_here), marks.reshape(ranges * own, blocks_here))

    weight_here = lax.dynamic_slice_in_dim(bed_weight, rank * cols_here, cols_here, 0)
    latest = forward_field[steps - 1]
    here = (adjoint_in[1] * latest[0] - adjoint_in[0] * latest[1]) * weight_here
    marks_here = lax.dynamic_slice_in_dim(labels, rank * blocks_here, blocks_here, 1)
    sums = sums + group_sums(block_sums(here), marks_here)

    sums = jnp.sum(lax.all_to_all(jnp.broadcast_to(sums, (ranges, GROUPS)), "dep", 0, 0), axis=0)
    sums = jnp.sum(lax.all_to_all(jnp.broadcast_to(sums, (sectors, GROUPS)), "az", 0, 0), axis=0)
    return (field, sums)


def solution(mesh):
    return jax.shard_map(
        on_device,
        mesh=mesh,
        in_specs=(
            P(None, "az", "dep"),
            P(None, None, "az", "dep"),
            P("az", "dep"),
            P(),
            P("az", None),
        ),
        out_specs=(P(None, "az", "dep"), P()),
        check_vma=False,
    )
```

time: 812 us -> 139 us (0.17)
  local copies, waits for them, and re-layouts: 281 us -> 20.7 us
  matrix products: 183 us -> 0 us
  blocking collectives: 189 us -> 12 us
  starting transfers between devices: 82 us -> 29.8 us
  other arithmetic: 36 us -> 11.8 us
  Pallas kernels: 0 us -> 23.2 us
  waiting for transfers between devices: 31.1 us -> 40.4 us
    dot_general x128 -> x0, matrix products: 183 us -> none  [the longest x32 50 us: combine(): jnp.einsum(form, imag_part, cosine, precision=highest)]
    unnamed x64 -> x20, local copies, waits for them, and re-layouts: 120 us -> 2.49 us
    all_to_all x12 -> x1, blocking collectives: 119 us -> 12 us  [on_device(): lax.all_to_all(jnp.broadcast_to(sums, (ranges, GROUPS)), 'dep', 0, 0)]
    psum x1 -> x0, blocking collectives: 70 us -> none  [on_device(): total = lax.psum(sensitivity, ('az', 'dep'))]
    ppermute x16 -> x2, starting transfers between devices: 65.3 us -> 4.21 us  [the longest x1 4.2 us: on_device(): above = lax.ppermute(stacked[:, rows_here - halo:], 'az', ahead)]
    all_to_all x17 -> x0, local copies, waits for them, and re-layouts: 45.1 us -> none  [the longest x9 42.7 us: on_device(): lax.all_to_all(propagate(deep), 'dep', split_axis=2, concat_axis=1, tiled...]
    div x8 -> x0, local copies, waits for them, and re-layouts: 34.9 us -> none  [propagate(): return jnp.stack([back_re, back_im]) / length]
    squeeze x32 -> x4, local copies, waits for them, and re-layouts: 39 us -> 5.58 us  [on_device(): here = (adjoint_in[1] * latest[0] - adjoint_in[0] * latest[1]) * weight_here]
  transfers between devices with their start and end apart: 20 -> 6, of which waited for: 16 -> 5; matrix products, arithmetic and copies ran while one was open for 7% -> 15% of each run, Pallas kernels for 0% -> 17%
where the time goes in v1:
time: 139 us
  waiting for transfers between devices  40.4 us (29%)
  starting transfers between devices  29.8 us (21%)
  Pallas kernels  23.2 us (17%)
  local copies, waits for them, and re-layouts  20.7 us (15%)
  blocking collectives  12 us (9%)
  other arithmetic  11.8 us (8%)
    pallas_call x1, Pallas kernels, run_steps(): pl.pallas_call(lambda *refs: steps_kernel(steps, halo, *refs), out_shape=...  23.2 us
    all_to_all x1, waiting for transfers between devices, on_device(): window = lax.all_to_all(windows, 'dep', 0, 0)  21.1 us
    all_to_all x1, starting transfers between devices, on_device(): lax.all_to_all(jnp.broadcast_to(sums, (sectors, GROUPS)), 'az', 0, 0)  12.4 us
    all_to_all x1, blocking collectives, on_device(): lax.all_to_all(jnp.broadcast_to(sums, (ranges, GROUPS)), 'dep', 0, 0)  12 us
    all_to_all x1, waiting for transfers between devices, on_device(): field = lax.all_to_all(final, 'dep', 0, 0)  8.11 us
    unnamed x7, other arithmetic  6.98 us
    all_to_all x1, waiting for transfers between devices, on_device(): lax.all_to_all(jnp.broadcast_to(sums, (sectors, GROUPS)), 'az', 0, 0)  6.15 us
    squeeze x4, local copies, waits for them, and re-layouts, on_device(): here = (adjoint_in[1] * latest[0] - adjoint_in[0] * latest[1]) * weight_here  5.58 us
  transfers between devices with their start and end apart: 6, of which 5 were waited for; matrix products, arithmetic and copies ran while one was open for 15% of the time, Pallas kernels for 17%

profile of v1, /device:TPU:1, one launch (start us, length us, event | category | flops | bytes accessed | tf_op | source)
XLA Modules:
  0.0 138.6 jit_solution(7547089114864942311)
XLA Ops:
  0.6 0.0 copy-start
  0.6 0.0 copy-start.7
  0.7 0.0 copy-start.6
  0.7 1.0 pad_maximum_fusion.4
  1.7 4.2 %collective-permute-start = (f32[3,16,512]{2,1,0:T(8,128)S(1)}, f32[3,16,512]{2,1,0:T(8,128)S(1)}, u32[]{:S(2)}, u32[]{:S(2)}) collective-permute-start(f32[3,16,512]{2,1,0:T(8,128)S(1)} %get-tuple-element.11), channel_id=1, source_target_pairs={{0,8},{8,16},{16,24},{24,32},{32,40},{40,48},{48,56},{56,64},{64,7... | collective-permute-start | bytes 294920 | tf_op jit(solution)/shard_map/ppermute | solution.py:285
  5.9 0.0 collective-permute-start.1
  5.9 1.6 %collective-permute-done = f32[3,16,512]{2,1,0:T(8,128)S(1)} collective-permute-done((f32[3,16,512]{2,1,0:T(8,128)S(1)}, f32[3,16,512]{2,1,0:T(8,128)S(1)}, u32[]{:S(2)}, u32[]{:S(2)}) %collective-permute-start) | collective-permute-done | bytes 98336 | tf_op jit(solution)/shard_map/ppermute | solution.py:285
  7.5 1.7 %fusion.21 = f32[8,3,48,512]{3,2,1,0:T(8,128)} fusion(f32[3,16,512]{2,1,0:T(8,128)S(1)} %collective-permute-done, f32[1,128,512]{2,1,0:T(8,128)} %bitcast.55, f32[2,128,512]{2,1,0:T(8,128)} %param.8), kind=kLoop, calls=%fused_computation.40 | loop fusion | flops 147455 | bytes 1179648
  9.2 0.0 copy-done.6
  9.2 1.6 %fusion.5 = f32[8,3,48,512]{3,2,1,0:T(8,128)} fusion(f32[8,3,48,512]{3,2,1,0:T(8,128)} %fusion.21, f32[2,128,512]{2,1,0:T(8,128)S(1)} %copy-done.6, f32[1,128,512]{2,1,0:T(8,128)} %bitcast.56), kind=kLoop, calls=%fused_computation.21 | loop fusion | flops 73728 | bytes 1081344
  10.8 0.0 copy-done.7
  10.8 0.7 fusion.8
  11.5 0.7 fusion.11
  12.3 0.7 fusion.14
  13.0 0.7 fusion.17
  13.7 0.7 fusion.2
  14.5 0.0 collective-permute-done.1
  14.5 0.7 fusion.19
  15.2 4.2 %all-to-all-start = ((f32[8,3,48,512]{3,2,1,0:T(8,128)}), f32[8,3,48,512]{3,2,1,0:T(8,128)S(1)}, u32[]{:S(2)}, u32[]{:S(2)}) async-start(f32[8,3,48,512]{3,2,1,0:T(8,128)} %fusion.19), calls=%async_computation | async-start | bytes 4718592 | tf_op jit(solution)/shard_map/all_to_all | solution.py:289
  19.5 0.0 slice-start
  19.5 2.0 %slice-done = f32[7,2,128,512]{3,2,1,0:T(8,128)S(1)} async-done(((f32[8,2,128,512]{3,2,1,0:T(8,128)}), f32[7,2,128,512]{3,2,1,0:T(8,128)S(1)}, s32[]{:S(2)}) %slice-start) | async-done | bytes 3670040 | tf_op jit(solution)/shard_map/slice | solution.py:291
  21.5 2.2 %copy.40 = f32[7,2,8,16,512]{4,3,1,0,2:T(8,128)} copy(f32[7,2,8,16,512]{4,3,2,1,0:T(8,128)S(1)} %bitcast.64) | data formatting | bytes 7340032 | tf_op jit(solution)/shard_map/reshape | solution.py:291
  23.6 21.1 %all-to-all-done.refs_0_ = f32[8,3,48,512]{3,2,1,0:T(8,128)S(1)} async-done(((f32[8,3,48,512]{3,2,1,0:T(8,128)}), f32[8,3,48,512]{3,2,1,0:T(8,128)S(1)}, u32[]{:S(2)}, u32[]{:S(2)}) %all-to-all-start) | async-done | bytes 2359328 | tf_op jit(solution)/shard_map/all_to_all | solution.py:289
  44.7 5.5 %all-to-all-start.2 = ((f32[8,7,2,16,512]{4,3,2,1,0:T(8,128)}), f32[8,7,2,16,512]{4,3,2,1,0:T(8,128)}, u32[]{:S(2)}, u32[]{:S(2)}) async-start(f32[8,7,2,16,512]{4,3,2,1,0:T(8,128)} %bitcast.63), calls=%async_computation.2 | async-start | bytes 7340032 | tf_op jit(solution)/shard_map/all_to_all | solution.py:292
  50.3 1.8 %fusion.23 = (f32[1,1,128,512]{3,2,1,0:T(8,128)}, f32[1,1,128,512]{3,2,1,0:T(8,128)}) fusion(f32[8,2,128,512]{3,2,1,0:T(8,128)} %param.9), kind=kLoop, calls=%fused_computation.53 | loop fusion | bytes 1048576 | tf_op jit(solution)/shard_map/slice | solution.py:308
  52.1 0.0 copy-start.3
  52.1 0.0 copy-start.4
  52.1 0.0 copy-start.5
  52.1 1.8 %squeeze.18 = f32[128,4,128]{2,1,0:T(4,128)} reshape(f32[1,1,128,512]{3,2,1,0:T(8,128)} %get-tuple-element.6) | data formatting | bytes 524288 | tf_op jit(solution)/shard_map/squeeze | solution.py:308
  53.9 0.8 fusion.25
  54.7 1.0 squeeze.19
  55.8 1.0 squeeze.20
  56.8 1.7 %squeeze.8 = f32[128,4,128]{2,1,0:T(4,128)} reshape(f32[1,128,512]{2,1,0:T(8,128)} %get-tuple-element.12) | data formatting | bytes 524288 | tf_op jit(solution)/shard_map/squeeze | solution.py:308
  58.5 0.8 dynamic-slice_bitcast_fusion
  59.3 1.2 multiply_reduce_fusion
  60.5 0.7 copy.33
  61.2 0.0 copy-done
  61.2 0.1 constant_dynamic-slice_fusion.1
  61.3 0.1 eq.28
  61.4 0.0 copy-done.3
  61.4 0.0 copy-done.4
  61.4 0.0 copy-done.5
  61.4 23.2 %steps.1 = (f32[8,7,2,16,512]{4,3,2,1,0:T(8,128)S(1)}, f32[8,2,16,512]{3,2,1,0:T(8,128)}) custom-call(f32[8,3,48,512]{3,2,1,0:T(8,128)S(1)} %all-to-all-done.refs_0_, bf16[2,256,256]{2,1,0:T(8,128)(2,1)S(1)} %copy-done.3, bf16[2,256,256]{2,1,0:T(8,128)(2,1)S(1)} %copy-done.4, f32[4,32,1,128]{3,2,1,0:T(1,128)S(1)} %copy-done.5), custom_call_target="tpu_custom_call" | custom-call | tf_op jit(solution)/shard_map/steps/pallas_call | solution.py:242
  84.6 0.0 copy-start.1
  84.6 1.9 %copy-done.1 = f32[8,7,2,16,512]{4,3,2,1,0:T(8,128)} copy-done((f32[8,7,2,16,512]{4,3,2,1,0:T(8,128)}, f32[8,7,2,16,512]{4,3,2,1,0:T(8,128)S(1)}, u32[]{:S(2)}) %copy-start.1) | copy-done | bytes 3670040
  86.5 3.4 %all-to-all-done.2 = f32[8,7,2,16,512]{4,3,2,1,0:T(8,128)} async-done(((f32[8,7,2,16,512]{4,3,2,1,0:T(8,128)}), f32[8,7,2,16,512]{4,3,2,1,0:T(8,128)}, u32[]{:S(2)}, u32[]{:S(2)}) %all-to-all-start.2) | async-done | bytes 3670048 | tf_op jit(solution)/shard_map/all_to_all | solution.py:292
  89.9 0.0 copy-start.2
  89.9 2.6 %fusion.24 = (f32[8,7,1,16,512]{4,3,2,1,0:T(8,128)S(1)}, f32[8,7,1,16,512]{4,3,2,1,0:T(8,128)S(1)}) fusion(f32[8,7,2,16,512]{4,3,2,1,0:T(8,128)} %all-to-all-done.2), kind=kLoop, calls=%fused_computation.54 | loop fusion | bytes 7340032 | tf_op jit(solution)/shard_map/slice | solution.py:299
  92.5 0.5 copy-done.2
  93.1 0.9 subtract_reduce_fusion
  94.0 0.1 reduce_sum.66
  94.1 0.0 copy-done.8
  94.1 0.2 multiply_reduce_fusion.1
  94.3 0.1 copy.38
  94.4 0.0 copy-done.9
  94.4 0.1 select_reduce_fusion
  94.5 12.0 %all_to_all.27 = f32[8,1,32]{2,1,0:T(1,128)S(1)} all-to-all(f32[8,1,32]{2,1,0:T(1,128)S(1)} %broadcast_in_dim.39), channel_id=1, replica_groups=mesh['az'=16,'dep'=8] {'dep'}, dimensions={0} | all-to-all | bytes 2048 | tf_op jit(solution)/shard_map/all_to_all | solution.py:312
  106.5 3.5 %all-to-all-start.1 = ((f32[8,2,16,512]{3,2,1,0:T(8,128)}), f32[8,2,16,512]{3,2,1,0:T(8,128)S(1)}, u32[]{:S(2)}, u32[]{:S(2)}) async-start(f32[8,2,16,512]{3,2,1,0:T(8,128)} %get-tuple-element.4), calls=%async_computation.1 | async-start | bytes 1048576 | tf_op jit(solution)/shard_map/all_to_all | solution.py:295
  110.0 8.1 %all-to-all-done.1 = f32[8,2,16,512]{3,2,1,0:T(8,128)S(1)} async-done(((f32[8,2,16,512]{3,2,1,0:T(8,128)}), f32[8,2,16,512]{3,2,1,0:T(8,128)S(1)}, u32[]{:S(2)}, u32[]{:S(2)}) %all-to-all-start.1) | async-done | bytes 524320 | tf_op jit(solution)/shard_map/all_to_all | solution.py:295
  118.1 0.6 broadcast_in_dim.40
  118.7 12.4 %all-to-all-start.4 = ((f32[16,1,32]{2,1,0:T(1,128)}), f32[16,1,32]{2,1,0:T(1,128)S(1)}, u32[]{:S(2)}, u32[]{:S(2)}) async-start(f32[16,1,32]{2,1,0:T(1,128)} %broadcast_in_dim.40), calls=%async_computation.4 | async-start | bytes 16384 | tf_op jit(solution)/shard_map/all_to_all | solution.py:313
  131.1 0.8 copy.28
  131.9 6.2 %all-to-all-done.4 = f32[16,1,32]{2,1,0:T(1,128)S(1)} async-done(((f32[16,1,32]{2,1,0:T(1,128)}), f32[16,1,32]{2,1,0:T(1,128)S(1)}, u32[]{:S(2)}, u32[]{:S(2)}) %all-to-all-start.4) | async-done | bytes 2080 | tf_op jit(solution)/shard_map/all_to_all | solution.py:313
  138.1 0.5 reduce_sum.72
  (7 shorter events, 0.0 us)
Async XLA Ops:
  0.6 60.6 %copy-start = (s32[128,32]{0,1:T(8,128)S(1)}, s32[128,32]{0,1:T(8,128)}, u32[]{:S(2)}) copy-start(s32[128,32]{0,1:T(8,128)} %param.12) | copy-start | bytes 49156
  0.6 10.2 %copy-start.7 = (f32[128,512]{1,0:T(8,128)S(1)}, f32[128,512]{1,0:T(8,128)}, u32[]{:S(2)}) copy-start(f32[128,512]{1,0:T(8,128)} %param.10) | copy-start | bytes 786436
  0.7 8.5 %copy-start.6 = (f32[2,128,512]{2,1,0:T(8,128)S(1)}, f32[2,128,512]{2,1,0:T(8,128)}, u32[]{:S(2)}) copy-start(f32[2,128,512]{2,1,0:T(8,128)} %param.8) | copy-start | bytes 1572868
  1.7 5.8 %collective-permute-start = (f32[3,16,512]{2,1,0:T(8,128)S(1)}, f32[3,16,512]{2,1,0:T(8,128)S(1)}, u32[]{:S(2)}, u32[]{:S(2)}) collective-permute-start(f32[3,16,512]{2,1,0:T(8,128)S(1)} %get-tuple-element.11), channel_id=1, source_target_pairs={{0,8},{8,16},{16,24},{24,32},{32,40},{40,48},{48,56},{56,64},{64,7... | collective-permute-start | bytes 294920 | tf_op jit(solution)/shard_map/ppermute | solution.py:285
  5.9 8.6 %collective-permute-start.1 = (f32[3,16,512]{2,1,0:T(8,128)S(1)}, f32[3,16,512]{2,1,0:T(8,128)S(1)}, u32[]{:S(2)}, u32[]{:S(2)}) collective-permute-start(f32[3,16,512]{2,1,0:T(8,128)S(1)} %get-tuple-element.10), channel_id=1, source_target_pairs={{8,0},{16,8},{24,16},{32,24},{40,32},{48,40},{56,48},{64,56},{72,6... | collective-permute-start | bytes 294920 | tf_op jit(solution)/shard_map/ppermute | solution.py:286
  15.2 29.5 %all-to-all-start = ((f32[8,3,48,512]{3,2,1,0:T(8,128)}), f32[8,3,48,512]{3,2,1,0:T(8,128)S(1)}, u32[]{:S(2)}, u32[]{:S(2)}) async-start(f32[8,3,48,512]{3,2,1,0:T(8,128)} %fusion.19), calls=%async_computation | async-start | bytes 4718592 | tf_op jit(solution)/shard_map/all_to_all | solution.py:289
  19.5 2.0 %slice-start = ((f32[8,2,128,512]{3,2,1,0:T(8,128)}), f32[7,2,128,512]{3,2,1,0:T(8,128)S(1)}, s32[]{:S(2)}) async-start(f32[8,2,128,512]{3,2,1,0:T(8,128)} %param.9), calls=%async_computation.5 | async-start | bytes 7340032 | tf_op jit(solution)/shard_map/slice | solution.py:291
  44.7 45.2 %all-to-all-start.2 = ((f32[8,7,2,16,512]{4,3,2,1,0:T(8,128)}), f32[8,7,2,16,512]{4,3,2,1,0:T(8,128)}, u32[]{:S(2)}, u32[]{:S(2)}) async-start(f32[8,7,2,16,512]{4,3,2,1,0:T(8,128)} %bitcast.63), calls=%async_computation.2 | async-start | bytes 7340032 | tf_op jit(solution)/shard_map/all_to_all | solution.py:292
  52.1 9.3 %copy-start.3 = (bf16[2,256,256]{2,1,0:T(8,128)(2,1)S(1)}, bf16[2,256,256]{2,1,0:T(8,128)(2,1)}, u32[]{:S(2)}) copy-start(bf16[2,256,256]{2,1,0:T(8,128)(2,1)} %constant.26.clone.refs_1_) | copy-start | bytes 786436
  52.1 9.3 %copy-start.4 = (bf16[2,256,256]{2,1,0:T(8,128)(2,1)S(1)}, bf16[2,256,256]{2,1,0:T(8,128)(2,1)}, u32[]{:S(2)}) copy-start(bf16[2,256,256]{2,1,0:T(8,128)(2,1)} %constant.27.clone.refs_2_) | copy-start | bytes 786436
  52.1 9.3 %copy-start.5 = (f32[4,32,1,128]{3,2,1,0:T(1,128)S(1)}, f32[4,32,1,128]{3,2,1,0:T(1,128)}, u32[]{:S(2)}) copy-start(f32[4,32,1,128]{3,2,1,0:T(1,128)} %constant.28.clone.refs_3_) | copy-start | bytes 196612
  84.6 1.9 %copy-start.1 = (f32[8,7,2,16,512]{4,3,2,1,0:T(8,128)}, f32[8,7,2,16,512]{4,3,2,1,0:T(8,128)S(1)}, u32[]{:S(2)}) copy-start(f32[8,7,2,16,512]{4,3,2,1,0:T(8,128)S(1)} %get-tuple-element.5) | copy-start | bytes 11010052
  89.9 3.1 %copy-start.2 = (f32[8,7,2,16,512]{4,3,2,1,0:T(8,128)S(1)}, f32[8,7,2,16,512]{4,3,2,1,0:T(8,128)}, u32[]{:S(2)}) copy-start(f32[8,7,2,16,512]{4,3,2,1,0:T(8,128)} %copy-done.1) | copy-start | bytes 11010052
  93.1 1.0 copy-start.8
  93.1 1.3 copy-start.9
  106.5 11.6 %all-to-all-start.1 = ((f32[8,2,16,512]{3,2,1,0:T(8,128)}), f32[8,2,16,512]{3,2,1,0:T(8,128)S(1)}, u32[]{:S(2)}, u32[]{:S(2)}) async-start(f32[8,2,16,512]{3,2,1,0:T(8,128)} %get-tuple-element.4), calls=%async_computation.1 | async-start | bytes 1048576 | tf_op jit(solution)/shard_map/all_to_all | solution.py:295
  118.7 19.3 %all-to-all-start.4 = ((f32[16,1,32]{2,1,0:T(1,128)}), f32[16,1,32]{2,1,0:T(1,128)S(1)}, u32[]{:S(2)}, u32[]{:S(2)}) async-start(f32[16,1,32]{2,1,0:T(1,128)} %broadcast_in_dim.40), calls=%async_computation.4 | async-start | bytes 16384 | tf_op jit(solution)/shard_map/all_to_all | solution.py:313

commit v2 on v1

--- a/solution.py
+++ b/solution.py
@@ -14,6 +14,12 @@
 LABEL_BLOCK = 128
 LANES = 128
 ROW_PAD = 8
+SCALARS = pl.BlockSpec(memory_space=pltpu.SMEM)
+IN_PLACE = pl.BlockSpec(memory_space=pltpu.HBM)
+
+
+def kept_out(value):
+    return pltpu.with_memory_space_constraint(value, pltpu.HBM)
 
 
 def split_table(table):
@@ -91,8 +97,17 @@
     return 2.0 * s * c, 1.0 - 2.0 * s * s
 
 
-def steps_kernel(steps, halo, window, ahead, back, tables, past, out, scr, angle_c, angle_s, mid, high, low):
-    outer, inner = mid.shape[1], mid.shape[2]
+def steps_kernel(steps, halo, rank, window, ahead_at, back_at, tables_at, past_at, *refs):
+    outer = window.shape[0]
+    pairs = refs[: outer // 2]
+    out, past, scr, angle_c, angle_s, mid, high, low, ahead, back, tables, arrived, left = refs[outer // 2 :]
+    copies = [
+        pltpu.make_async_copy(source, target, arrived.at[number])
+        for number, (source, target) in enumerate(((ahead_at, ahead), (back_at, back), (tables_at, tables)))
+    ]
+    for copy in copies:
+        copy.start()
+    inner = mid.shape[2]
     blocks = outer * inner
     rows = window.shape[2]
     own = rows - 2 * halo
@@ -120,6 +135,8 @@
         return carry
 
     lax.fori_loop(0, outer, start, 0)
+    for copy in copies:
+        copy.wait()
 
     def couple(p, q, base):
         def at(part, shift):
@@ -205,9 +222,12 @@
                             if last:
                                 out[p, part, centre, lanes] = turned[p][part]
                             else:
-                                past[p, index, part, centre, lanes] = turned[p][part]
+                                past[index, p, part, centre, lanes] = turned[p][part]
                     if not last:
                         turn_screen(turned[p], p, q, base)
+
+    def leave(at):
+        return pltpu.make_async_copy(past.at[at], past_at.at[at], left.at[at])
 
     spans = []
     for index in range(steps):
@@ -226,91 +246,234 @@
 
         def run(at, carry, span=spans[index]):
             step(at, *span, False)
+            leave(at).start()
             return carry
 
         lax.fori_loop(index, stop, run, 0)
         index = stop
-
-
-def run_steps(window, steps, halo):
+    for number, pair in enumerate(pairs):
+        for side in range(2):
+            pair[side] = out[rank[0] ^ (2 * number + side)]
+    for at in range(steps - 1):
+        leave(at).wait()
+
+
+def run_steps(window, rank, steps, halo):
     sources, _, rows, cols = window.shape
     inner = cols // LANES
     ahead, back, tables = transform_tables(sources * cols)
     own = rows - 2 * halo
     vmem = pl.BlockSpec(memory_space=pltpu.VMEM)
     field = (sources, inner)
-    return pl.pallas_call(
+    result = pl.pallas_call(
         lambda *refs: steps_kernel(steps, halo, *refs),
-        out_shape=(
-            jax.ShapeDtypeStruct((sources, steps - 1, 2, own, cols), jnp.float32),
-            jax.ShapeDtypeStruct((sources, 2, own, cols), jnp.float32),
-        ),
-        in_specs=[vmem] * 4,
-        out_specs=(vmem, vmem),
+        out_shape=[pltpu.HBM((steps - 1, sources, 2, own, cols), jnp.float32)]
+        + [jax.ShapeDtypeStruct((2, 2, own, cols), jnp.float32)] * (sources // 2),
+        in_specs=[SCALARS, vmem] + [IN_PLACE] * 3,
+        out_specs=[IN_PLACE] + [vmem] * (sources // 2),
         scratch_shapes=[
+            pltpu.VMEM((sources, 2, own, cols), jnp.float32),
+            pltpu.VMEM((steps - 1, sources, 2, own, cols), jnp.float32),
             pltpu.VMEM((2,) + field + (rows + 2 * ROW_PAD, LANES), jnp.float32),
             pltpu.VMEM(field + (rows, LANES), jnp.float32),
             pltpu.VMEM(field + (rows, LANES), jnp.float32),
             pltpu.VMEM((2,) + field + (rows, LANES), jnp.float32),
             pltpu.VMEM(field + (rows, 2 * LANES), jnp.bfloat16),
             pltpu.VMEM(field + (rows, 2 * LANES), jnp.bfloat16),
+            pltpu.VMEM(ahead.shape, jnp.bfloat16),
+            pltpu.VMEM(back.shape, jnp.bfloat16),
+            pltpu.VMEM(tables.shape, jnp.float32),
+            pltpu.SemaphoreType.DMA((3,)),
+            pltpu.SemaphoreType.DMA((steps - 1,)),
         ],
-        compiler_params=pltpu.CompilerParams(vmem_limit_bytes=40 * 1024 * 1024),
+        compiler_params=pltpu.CompilerParams(vmem_limit_bytes=20 * 1024 * 1024),
+        cost_estimate=pl.CostEstimate(flops=20_000_000_000, transcendentals=0, bytes_accessed=8_000_000),
         name="steps",
-    )(window, jnp.asarray(ahead), jnp.asarray(back), jnp.asarray(tables))
-
-
-def group_sums(blocks, marks):
-    hit = marks[:, :, None] == jnp.arange(GROUPS, dtype=jnp.int32)
-    return jnp.sum(jnp.where(hit, blocks[:, :, None], 0.0), axis=(0, 1))
-
-
-def block_sums(term):
-    return term.reshape(term.shape[:-1] + (-1, LABEL_BLOCK)).sum(-1)
+    )(rank, window, *[kept_out(jnp.asarray(table)) for table in (ahead, back, tables)])
+    return result[0], result[1:]
+
+
+def windows_kernel(own, halo, field, screen, above, below, out):
+    rows = screen.shape[0]
+    for target in range(rows // own):
+        first = target * own - halo
+        for row in range(first, first + own + 2 * halo, own):
+            to = slice(row - first, row - first + own)
+            for part in range(3):
+                if row < 0:
+                    out[target, part, to] = above[part]
+                elif row >= rows:
+                    out[target, part, to] = below[part]
+                elif part < 2:
+                    out[target, part, to] = field[part, row : row + own]
+                else:
+                    out[target, part, to] = screen[row : row + own]
+
+
+def make_windows(field, screen, above, below, own, halo):
+    rows, cols = screen.shape
+    vmem = pl.BlockSpec(memory_space=pltpu.VMEM)
+    return pl.pallas_call(
+        lambda *refs: windows_kernel(own, halo, *refs),
+        out_shape=jax.ShapeDtypeStruct((rows // own, 3, own + 2 * halo, cols), jnp.float32),
+        in_specs=[vmem] * 4,
+        out_specs=vmem,
+        compiler_params=pltpu.CompilerParams(vmem_limit_bytes=4 * 1024 * 1024),
+        name="windows",
+    )(field, screen, above, below)
+
+
+def add_groups(total, term, marks):
+    lane = lax.broadcasted_iota(jnp.int32, total.shape, 1)
+    for block in range(term.shape[1] // LABEL_BLOCK):
+        part = jnp.sum(term[:, block * LABEL_BLOCK : (block + 1) * LABEL_BLOCK], axis=1, keepdims=True)
+        total = total + jnp.where(marks[:, block : block + 1] == lane, part, 0.0)
+    return total
+
+
+def here_kernel(rank, field, latest, weight, marks, out):
+    total = jnp.zeros((8, LANES), jnp.float32)
+    for row in range(0, field.shape[1], 8):
+        at = slice(row, row + 8)
+        term = (field[1, at] * latest[0, 0, at] - field[0, at] * latest[0, 1, at]) * weight[rank[0]]
+        total = add_groups(total, term, marks[at])
+    out[...] = total
+
+
+def sums_here(rank, field, forward_field, weight, marks):
+    steps, _, rows, cols = forward_field.shape
+    vmem = pl.BlockSpec(memory_space=pltpu.VMEM)
+    return pl.pallas_call(
+        here_kernel,
+        out_shape=jax.ShapeDtypeStruct((8, LANES), jnp.float32),
+        grid=(1,),
+        in_specs=[
+            SCALARS,
+            vmem,
+            pl.BlockSpec((1, 2, rows, cols), lambda i: (steps - 1, 0, 0, 0)),
+            vmem,
+            vmem,
+        ],
+        out_specs=vmem,
+        compiler_params=pltpu.CompilerParams(vmem_limit_bytes=8 * 1024 * 1024),
+        cost_estimate=pl.CostEstimate(flops=2_000_000_000, transcendentals=0, bytes_accessed=1_000_000),
+        name="here",
+    )(rank, field, forward_field, weight, marks)
+
+
+def sums_kernel(past_at, stored_at, weight, marks, here, out, past, stored, arrived):
+    steps, sources, _, own, _ = past.shape
+    copies = []
+    for source in range(sources):
+        copies.append(
+            (
+                pltpu.make_async_copy(stored_at.at[source], stored.at[source], arrived.at[0, source]),
+                pltpu.make_async_copy(past_at.at[:, source], past.at[:, source], arrived.at[1, source]),
+            )
+        )
+    for pair in copies:
+        for copy in pair:
+            copy.start()
+    total = here[...]
+    for source, pair in enumerate(copies):
+        for copy in pair:
+            copy.wait()
+        for row in range(0, own, 8):
+            at = slice(row, row + 8)
+            term = None
+            for index in range(steps):
+                kept = steps - 1 - index
+                one = past[index, source, 1, at] * stored[source, kept, 0, at]
+                two = past[index, source, 0, at] * stored[source, kept, 1, at]
+                term = one - two if term is None else term + (one - two)
+            total = add_groups(total, term * weight[source], marks[source, at])
+    out[...] = jnp.sum(total, axis=0, keepdims=True)
+
+
+def group_sums(past, stored, weight, marks, here):
+    vmem = pl.BlockSpec(memory_space=pltpu.VMEM)
+    return pl.pallas_call(
+        sums_kernel,
+        out_shape=jax.ShapeDtypeStruct((1, LANES), jnp.float32),
+        in_specs=[IN_PLACE] * 2 + [vmem] * 3,
+        out_specs=vmem,
+        scratch_shapes=[
+            pltpu.VMEM(past.shape, jnp.float32),
+            pltpu.VMEM(stored.shape, jnp.float32),
+            pltpu.SemaphoreType.DMA((2, past.shape[1])),
+        ],
+        compiler_params=pltpu.CompilerParams(vmem_limit_bytes=10 * 1024 * 1024),
+        name="sums",
+    )(kept_out(past), kept_out(stored), weight, marks, here)
+
+
+def gather_kernel(rank, across, *refs):
+    pairs, out = refs[:-1], refs[-1]
+    own = across.shape[2]
+    for number, pair in enumerate(pairs):
+        for side, piece in enumerate((pair[0], across[number])):
+            row = pl.multiple_of((rank[0] ^ (2 * number + side)) * own, own)
+            out[:, pl.ds(row, own)] = piece
+
+
+def gather_rows(rank, across, pairs):
+    _, _, own, cols = across.shape
+    vmem = pl.BlockSpec(memory_space=pltpu.VMEM)
+    return pl.pallas_call(
+        gather_kernel,
+        out_shape=jax.ShapeDtypeStruct((2, 2 * own * len(pairs), cols), jnp.float32),
+        in_specs=[SCALARS] + [vmem] * (1 + len(pairs)),
+        out_specs=vmem,
+        compiler_params=pltpu.CompilerParams(vmem_limit_bytes=8 * 1024 * 1024),
+        name="gather",
+    )(rank, across, *pairs)
+
+
+def swap(value, other, count):
+    return lax.ppermute(value, "dep", [(i, i ^ other) for i in range(count)])
 
 
 def on_device(adjoint_in, forward_field, screen, bed_weight, labels):
     steps = forward_field.shape[0]
     sectors = lax.axis_size("az")
     ranges = lax.axis_size("dep")
-    rank = lax.axis_index("dep")
+    position = lax.axis_index("dep")
+    rank = position.reshape(1)
     rows_here, cols_here = screen.shape
     own = rows_here // ranges
     halo = 2 * steps
     blocks_here = cols_here // LABEL_BLOCK
 
-    stacked = jnp.concatenate([adjoint_in, screen[None]])
+    def edge(rows):
+        return jnp.concatenate([adjoint_in[:, rows], screen[None, rows]])
+
     ahead = [(i, (i + 1) % sectors) for i in range(sectors)]
     behind = [((i + 1) % sectors, i) for i in range(sectors)]
-    above = lax.ppermute(stacked[:, rows_here - halo :], "az", ahead)
-    below = lax.ppermute(stacked[:, :halo], "az", behind)
-    wide = jnp.concatenate([above, stacked, below], axis=1)
-    windows = jnp.stack([wide[:, d * own : (d + 1) * own + 2 * halo] for d in range(ranges)])
+    above = lax.ppermute(edge(slice(rows_here - halo, rows_here)), "az", ahead)
+    below = lax.ppermute(edge(slice(0, halo)), "az", behind)
+
+    windows = make_windows(adjoint_in, screen, above, below, own, halo)
     window = lax.all_to_all(windows, "dep", 0, 0)
 
+    weight = bed_weight.reshape(ranges, 1, cols_here)
+    marks_here = lax.dynamic_slice_in_dim(labels, position * blocks_here, blocks_here, 1)
+    here = sums_here(rank, adjoint_in, forward_field, weight, marks_here)
+    marks = lax.dynamic_slice_in_dim(labels, position * own, own, 0)
+    marks = jnp.transpose(marks.reshape(own, ranges, blocks_here), (1, 0, 2))
+
     stored = forward_field[: steps - 1].reshape(steps - 1, 2, ranges, own, cols_here)
-    stored = lax.all_to_all(jnp.transpose(stored, (2, 0, 1, 3, 4)), "dep", 0, 0)
-
-    past, final = run_steps(window, steps, halo)
-    field = lax.all_to_all(final, "dep", 0, 0)
-    field = jnp.transpose(field, (1, 0, 2, 3)).reshape(2, rows_here, cols_here)
-
-    stored = stored[:, ::-1]
-    term = jnp.sum(past[:, :, 1] * stored[:, :, 0] - past[:, :, 0] * stored[:, :, 1], axis=1)
-    term = term * bed_weight.reshape(ranges, 1, cols_here)
-    marks = lax.dynamic_slice_in_dim(labels, rank * own, own, 0)
-    blocks = block_sums(term)
-    marks = jnp.transpose(marks.reshape(own, ranges, blocks_here), (1, 0, 2))
-    sums = group_sums(blocks.reshape(ranges * own, blocks_here), marks.reshape(ranges * own, blocks_here))
-
-    weight_here = lax.dynamic_slice_in_dim(bed_weight, rank * cols_here, cols_here, 0)
-    latest = forward_field[steps - 1]
-    here = (adjoint_in[1] * latest[0] - adjoint_in[0] * latest[1]) * weight_here
-    marks_here = lax.dynamic_slice_in_dim(labels, rank * blocks_here, blocks_here, 1)
-    sums = sums + group_sums(block_sums(here), marks_here)
-
-    sums = jnp.sum(lax.all_to_all(jnp.broadcast_to(sums, (ranges, GROUPS)), "dep", 0, 0), axis=0)
-    sums = jnp.sum(lax.all_to_all(jnp.broadcast_to(sums, (sectors, GROUPS)), "az", 0, 0), axis=0)
+    stored = jnp.transpose(stored, (2, 0, 1, 3, 4))
+    window, here, marks, stored = lax.optimization_barrier((window, here, marks, stored))
+    stored = lax.all_to_all(stored, "dep", 0, 0)
+
+    past, pairs = run_steps(window, rank, steps, halo)
+    pairs = [pairs[0]] + [swap(pairs[number], 2 * number, ranges) for number in range(1, ranges // 2)]
+    sums = group_sums(past, stored, weight, marks, here)
+    _, *ready = lax.optimization_barrier((sums, *pairs))
+    across = jnp.stack([pair[1] for pair in ready])
+    field = gather_rows(rank, swap(across, 1, ranges), ready)
+    sums = jnp.broadcast_to(sums[None, 0, :GROUPS], (sectors * ranges, GROUPS))
+    sums = jnp.sum(lax.all_to_all(sums, ("az", "dep"), 0, 0), axis=0)
     return (field, sums)
 
 

time: 139 us -> 124 us (0.89)
  starting transfers between devices: 29.8 us -> 17.8 us
  other arithmetic: 11.8 us -> 0.7 us
  local copies, waits for them, and re-layouts: 20.7 us -> 9.71 us
  blocking collectives: 12 us -> 19.8 us
  Pallas kernels: 23.2 us -> 28.9 us
  waiting for transfers between devices: 40.4 us -> 45.8 us
    all_to_all x3 -> x1, starting transfers between devices: 21.4 us -> 4.49 us  [on_device(): stored = lax.all_to_all(stored, 'dep', 0, 0)]
    all_to_all x1, blocking collectives: 12 us -> 19.8 us  [on_device(): sums = jnp.sum(lax.all_to_all(sums, ('az', 'dep'), 0, 0), axis=0)]
    unnamed x7 -> x0, other arithmetic: 6.98 us -> none
    pallas_call x0 -> x4, Pallas kernels: none -> 6.13 us  [the longest x1 3.39 us: group_sums(): pl.pallas_call(sums_kernel, out_shape=jax.ShapeDtypeStruct((1, LANES), jn...]
    squeeze x4 -> x0, local copies, waits for them, and re-layouts: 5.58 us -> none  [on_device(): here = (adjoint_in[1] * latest[0] - adjoint_in[0] * latest[1]) * weight_here]
    ppermute x2 -> x6, waiting for transfers between devices: 1.64 us -> 6.55 us  [the longest x1 3.98 us: on_device(): below = lax.ppermute(edge(slice(0, halo)), 'az', behind)]
    ppermute x2 -> x6, starting transfers between devices: 4.21 us -> 9.08 us  [the longest x4 4.8 us: swap(): return lax.ppermute(value, 'dep', [(i, i ^ other) for i in range(count)])]
    slice x3 -> x6, local copies, waits for them, and re-layouts: 5.27 us -> 0.91 us  [the longest x1 0.88 us: edge(): return jnp.concatenate([adjoint_in[:, rows], screen[None, rows]])]
  transfers between devices with their start and end apart: 6 -> 8, of which waited for: 5 -> 6; matrix products, arithmetic and copies ran while one was open for 15% -> 3% of each run, Pallas kernels for 17% -> 21%
where the time goes in v2:
time: 124 us; the launch traced here: 123 us
  waiting for transfers between devices  45.8 us (37%)
  Pallas kernels  28.9 us (23%)
  blocking collectives  19.8 us (16%)
  starting transfers between devices  17.8 us (14%)
  local copies, waits for them, and re-layouts  9.71 us (8%)
    all_to_all x1, waiting for transfers between devices, on_device(): window = lax.all_to_all(windows, 'dep', 0, 0)  22.9 us
    pallas_call x1, Pallas kernels, run_steps(): pl.pallas_call(lambda *refs: steps_kernel(steps, halo, *refs), out_shape=...  22.7 us
    all_to_all x1, blocking collectives, on_device(): sums = jnp.sum(lax.all_to_all(sums, ('az', 'dep'), 0, 0), axis=0)  19.8 us
    all_to_all x1, waiting for transfers between devices, on_device(): stored = lax.all_to_all(stored, 'dep', 0, 0)  16.3 us
    ppermute x4, starting transfers between devices, swap(): return lax.ppermute(value, 'dep', [(i, i ^ other) for i in range(count)])  4.8 us
    all_to_all x1, starting transfers between devices, on_device(): stored = lax.all_to_all(stored, 'dep', 0, 0)  4.49 us
    all_to_all x1, starting transfers between devices, on_device(): window = lax.all_to_all(windows, 'dep', 0, 0)  4.22 us
    ppermute x1, starting transfers between devices, on_device(): above = lax.ppermute(edge(slice(rows_here - halo, rows_here)), 'az', ahead)  4.2 us
  transfers between devices with their start and end apart: 8, of which 6 were waited for; matrix products, arithmetic and copies ran while one was open for 3% of the time, Pallas kernels for 21%

profile of v2, /device:TPU:1, one launch (start us, length us, event | category | flops | bytes accessed | tf_op | source)
XLA Modules:
  0.0 123.4 jit_solution(3553701728726629811)
XLA Ops:
  0.6 0.0 copy-start
  0.6 0.8 slice_bitcast_fusion
  1.4 0.9 fusion
  2.3 4.2 %collective-permute-start = (f32[3,16,512]{2,1,0:T(8,128)S(1)}, f32[3,16,512]{2,1,0:T(8,128)S(1)}, u32[]{:S(2)}, u32[]{:S(2)}) collective-permute-start(f32[3,16,512]{2,1,0:T(8,128)S(1)} %pad_maximum_fusion.1), channel_id=1, source_target_pairs={{0,8},{8,16},{16,24},{24,32},{32,40},{40,48},{48,56},{56,64},{64,7... | collective-permute-start | bytes 294920 | tf_op jit(solution)/shard_map/ppermute | solution.py:452
  6.5 0.1 collective-permute-start.1
  6.6 1.6 %collective-permute-done.refs_2_ = f32[3,16,512]{2,1,0:T(8,128)S(1)} collective-permute-done((f32[3,16,512]{2,1,0:T(8,128)S(1)}, f32[3,16,512]{2,1,0:T(8,128)S(1)}, u32[]{:S(2)}, u32[]{:S(2)}) %collective-permute-start) | collective-permute-done | bytes 98336 | tf_op jit(solution)/shard_map/ppermute | solution.py:452
  8.2 4.0 %collective-permute-done.1.refs_3_ = f32[3,16,512]{2,1,0:T(8,128)S(1)} collective-permute-done((f32[3,16,512]{2,1,0:T(8,128)S(1)}, f32[3,16,512]{2,1,0:T(8,128)S(1)}, u32[]{:S(2)}, u32[]{:S(2)}) %collective-permute-start.1) | collective-permute-done | bytes 98336 | tf_op jit(solution)/shard_map/ppermute | solution.py:453
  12.2 0.0 copy-start.2
  12.2 1.0 copy-done.2
  13.2 0.0 copy-start.4
  13.2 0.9 copy-done.4
  14.1 1.5 %windows.1 = f32[8,3,48,512]{3,2,1,0:T(8,128)} custom-call(f32[2,128,512]{2,1,0:T(8,128)S(1)} %copy-done.2, f32[128,512]{1,0:T(8,128)S(1)} %copy-done.4, f32[3,16,512]{2,1,0:T(8,128)S(1)} %collective-permute-done.refs_2_, f32[3,16,512]{2,1,0:T(8,128)S(1)} %collective-permute-done.1.refs_3_), custom_call_target="tpu_custom_call" | custom-call | tf_op jit(solution)/shard_map/windows/pallas_call | solution.py:316
  15.7 4.2 %all-to-all-start = ((f32[8,3,48,512]{3,2,1,0:T(8,128)}), f32[8,3,48,512]{3,2,1,0:T(8,128)S(1)}, u32[]{:S(2)}, u32[]{:S(2)}) async-start(f32[8,3,48,512]{3,2,1,0:T(8,128)} %windows.1), calls=%async_computation | async-start | bytes 4718592 | tf_op jit(solution)/shard_map/all_to_all | solution.py:456
  19.9 0.0 copy-done
  19.9 0.1 constant_dynamic-slice_fusion
  20.0 0.1 copy.18
  20.1 0.1 copy.22.marks
  20.2 0.0 slice-start
  20.3 2.0 %slice-done = f32[7,2,128,512]{3,2,1,0:T(8,128)S(1)} async-done(((f32[8,2,128,512]{3,2,1,0:T(8,128)}), f32[7,2,128,512]{3,2,1,0:T(8,128)S(1)}, s32[]{:S(2)}) %slice-start) | async-done | bytes 3670040 | tf_op jit(solution)/shard_map/slice | solution.py:464
  22.3 0.0 copy-start.1
  22.3 0.0 copy-start.3
  22.3 0.0 copy-start.5
  22.3 2.2 %copy.24 = f32[7,2,8,16,512]{4,3,1,0,2:T(8,128)} copy(f32[7,2,8,16,512]{4,3,2,1,0:T(8,128)S(1)} %bitcast.14) | data formatting | bytes 7340032 | tf_op jit(solution)/shard_map/reshape | solution.py:464
  24.5 1.3 %copy-done.1 = f32[8,2,128,512]{3,2,1,0:T(8,128)S(1)} copy-done((f32[8,2,128,512]{3,2,1,0:T(8,128)S(1)}, f32[8,2,128,512]{3,2,1,0:T(8,128)}, u32[]{:S(2)}) %copy-start.1) | copy-done | bytes 4194328
  25.8 0.1 copy-done.3
  25.9 0.0 copy-done.5
  25.9 0.4 here.1
  26.3 22.9 %all-to-all-done.refs_1_ = f32[8,3,48,512]{3,2,1,0:T(8,128)S(1)} async-done(((f32[8,3,48,512]{3,2,1,0:T(8,128)}), f32[8,3,48,512]{3,2,1,0:T(8,128)S(1)}, u32[]{:S(2)}, u32[]{:S(2)}) %all-to-all-start) | async-done | bytes 2359328 | tf_op jit(solution)/shard_map/all_to_all | solution.py:456
  49.2 4.5 %all-to-all-start.1 = ((f32[8,7,2,16,512]{4,3,2,1,0:T(8,128)}), f32[8,7,2,16,512]{4,3,2,1,0:T(8,128)}, u32[]{:S(2)}, u32[]{:S(2)}) async-start(f32[8,7,2,16,512]{4,3,2,1,0:T(8,128)} %bitcast.18), calls=%async_computation.1 | async-start | bytes 7340032 | tf_op jit(solution)/shard_map/all_to_all | solution.py:467
  53.7 22.7 %steps.1 = (f32[7,8,2,16,512]{4,3,2,1,0:T(8,128)}, f32[2,2,16,512]{3,2,1,0:T(8,128)S(1)}, f32[2,2,16,512]{3,2,1,0:T(8,128)S(1)}, f32[2,2,16,512]{3,2,1,0:T(8,128)S(1)}, f32[2,2,16,512]{3,2,1,0:T(8,128)S(1)}) custom-call(s32[1]{0:T(128)} %bitcast.rank.refs_0_, f32[8,3,48,512]{3,2,1,0:T(8,128)S(1)} %all-to-all-done.refs_1_, ...), custom_call_target="tpu_custom_call" | custom-call | flops 20000000000 | bytes 8000000 | tf_op jit(solution)/shard_map/steps/pallas_call | solution.py:268
  76.4 1.4 %collective-permute-start.2 = (f32[2,2,16,512]{3,2,1,0:T(8,128)S(1)}, f32[2,2,16,512]{3,2,1,0:T(8,128)S(1)}, u32[]{:S(2)}, u32[]{:S(2)}) collective-permute-start(f32[2,2,16,512]{3,2,1,0:T(8,128)S(1)} %get-tuple-element.21), channel_id=1, source_target_pairs={{0,2},{1,3},{2,0},{3,1},{4,6},{5,7},{6,4},{7,5},{8,10},{9,11},{10,... | collective-permute-start | bytes 393224 | tf_op jit(solution)/shard_map/ppermute | solution.py:433
  77.9 2.4 %collective-permute-start.3 = (f32[2,2,16,512]{3,2,1,0:T(8,128)S(1)}, f32[2,2,16,512]{3,2,1,0:T(8,128)S(1)}, u32[]{:S(2)}, u32[]{:S(2)}) collective-permute-start(f32[2,2,16,512]{3,2,1,0:T(8,128)S(1)} %get-tuple-element.22), channel_id=1, source_target_pairs={{0,4},{1,5},{2,6},{3,7},{4,0},{5,1},{6,2},{7,3},{8,12},{9,13},{10,... | collective-permute-start | bytes 393224 | tf_op jit(solution)/shard_map/ppermute | solution.py:433
  80.3 0.1 collective-permute-start.4
  80.4 16.3 %all-to-all-done.1.stored_at = f32[8,7,2,16,512]{4,3,2,1,0:T(8,128)} async-done(((f32[8,7,2,16,512]{4,3,2,1,0:T(8,128)}), f32[8,7,2,16,512]{4,3,2,1,0:T(8,128)}, u32[]{:S(2)}, u32[]{:S(2)}) %all-to-all-start.1) | async-done | bytes 3670048 | tf_op jit(solution)/shard_map/all_to_all | solution.py:467
  96.7 3.4 %sums.1 = f32[1,128]{1,0:T(1,128)S(1)} custom-call(f32[7,8,2,16,512]{4,3,2,1,0:T(8,128)} %get-tuple-element.16.past_at, f32[8,7,2,16,512]{4,3,2,1,0:T(8,128)} %all-to-all-done.1.stored_at, f32[8,1,512]{2,1,0:T(1,128)S(1)} %bitcast.17, s32[8,16,4]{2,1,0:T(8,128)S(1)} %bitcast.15, f32[8,128]{1,0:T(8,128)S(1)} %here.1), custom_call_target="tpu_custom_call" | custom-call | tf_op jit(solution)/shard_map/sums/pallas_call | solution.py:395
  100.1 0.0 collective-permute-done.2.refs_1_
  100.1 0.6 collective-permute-done.3.refs_2_
  100.7 0.4 collective-permute-done.4.refs_3_
  101.2 0.9 collective-permute-start.5
  102.1 19.8 %all_to_all.16 = f32[128,1,32]{2,1,0:T(1,128)S(1)} all-to-all(f32[128,1,32]{2,1,0:T(1,128)S(1)} %broadcast_in_dim.13), channel_id=1, replica_groups=mesh['az'=16,'dep'=8] {'az','dep'}, dimensions={0} | all-to-all | bytes 32768 | tf_op jit(solution)/shard_map/all_to_all | solution.py:476
  121.9 0.7 reduce_sum.9
  122.6 0.0 collective-permute-done.5.across
  122.6 0.8 gather.1
  (10 shorter events, 0.1 us)
Async XLA Ops:
  0.6 19.3 %copy-start = (s32[128,32]{0,1:T(8,128)S(1)}, s32[128,32]{0,1:T(8,128)}, u32[]{:S(2)}) copy-start(s32[128,32]{0,1:T(8,128)} %param.12) | copy-start | bytes 49156
  2.3 5.8 %collective-permute-start = (f32[3,16,512]{2,1,0:T(8,128)S(1)}, f32[3,16,512]{2,1,0:T(8,128)S(1)}, u32[]{:S(2)}, u32[]{:S(2)}) collective-permute-start(f32[3,16,512]{2,1,0:T(8,128)S(1)} %pad_maximum_fusion.1), channel_id=1, source_target_pairs={{0,8},{8,16},{16,24},{24,32},{32,40},{40,48},{48,56},{56,64},{64,7... | collective-permute-start | bytes 294920 | tf_op jit(solution)/shard_map/ppermute | solution.py:452
  6.5 5.6 %collective-permute-start.1 = (f32[3,16,512]{2,1,0:T(8,128)S(1)}, f32[3,16,512]{2,1,0:T(8,128)S(1)}, u32[]{:S(2)}, u32[]{:S(2)}) collective-permute-start(f32[3,16,512]{2,1,0:T(8,128)S(1)} %pad_maximum_fusion.2), channel_id=1, source_target_pairs={{8,0},{16,8},{24,16},{32,24},{40,32},{48,40},{56,48},{64,56},{72,6... | collective-permute-start | bytes 294920 | tf_op jit(solution)/shard_map/ppermute | solution.py:453
  12.2 1.0 copy-start.2
  13.2 0.9 copy-start.4
  15.7 33.5 %all-to-all-start = ((f32[8,3,48,512]{3,2,1,0:T(8,128)}), f32[8,3,48,512]{3,2,1,0:T(8,128)S(1)}, u32[]{:S(2)}, u32[]{:S(2)}) async-start(f32[8,3,48,512]{3,2,1,0:T(8,128)} %windows.1), calls=%async_computation | async-start | bytes 4718592 | tf_op jit(solution)/shard_map/all_to_all | solution.py:456
  20.2 2.0 %slice-start = ((f32[8,2,128,512]{3,2,1,0:T(8,128)}), f32[7,2,128,512]{3,2,1,0:T(8,128)S(1)}, s32[]{:S(2)}) async-start(f32[8,2,128,512]{3,2,1,0:T(8,128)} %latest.1), calls=%async_computation.3 | async-start | bytes 7340032 | tf_op jit(solution)/shard_map/slice | solution.py:464
  22.3 3.5 %copy-start.1 = (f32[8,2,128,512]{3,2,1,0:T(8,128)S(1)}, f32[8,2,128,512]{3,2,1,0:T(8,128)}, u32[]{:S(2)}) copy-start(f32[8,2,128,512]{3,2,1,0:T(8,128)} %latest.1) | copy-start | bytes 12582916
  22.3 3.6 %copy-start.3 = (f32[2,128,512]{2,1,0:T(8,128)S(1)}, f32[2,128,512]{2,1,0:T(8,128)}, u32[]{:S(2)}) copy-start(f32[2,128,512]{2,1,0:T(8,128)} %field.1) | copy-start | bytes 1572868
  22.3 3.6 %copy-start.5 = (f32[4096]{0:T(1024)S(1)}, f32[4096]{0:T(1024)}, u32[]{:S(2)}) copy-start(f32[4096]{0:T(1024)} %param.11) | copy-start | bytes 49156
  49.2 47.5 %all-to-all-start.1 = ((f32[8,7,2,16,512]{4,3,2,1,0:T(8,128)}), f32[8,7,2,16,512]{4,3,2,1,0:T(8,128)}, u32[]{:S(2)}, u32[]{:S(2)}) async-start(f32[8,7,2,16,512]{4,3,2,1,0:T(8,128)} %bitcast.18), calls=%async_computation.1 | async-start | bytes 7340032 | tf_op jit(solution)/shard_map/all_to_all | solution.py:467
  76.4 23.6 %collective-permute-start.2 = (f32[2,2,16,512]{3,2,1,0:T(8,128)S(1)}, f32[2,2,16,512]{3,2,1,0:T(8,128)S(1)}, u32[]{:S(2)}, u32[]{:S(2)}) collective-permute-start(f32[2,2,16,512]{3,2,1,0:T(8,128)S(1)} %get-tuple-element.21), channel_id=1, source_target_pairs={{0,2},{1,3},{2,0},{3,1},{4,6},{5,7},{6,4},{7,5},{8,10},{9,11},{10,... | collective-permute-start | bytes 393224 | tf_op jit(solution)/shard_map/ppermute | solution.py:433
  77.9 22.8 %collective-permute-start.3 = (f32[2,2,16,512]{3,2,1,0:T(8,128)S(1)}, f32[2,2,16,512]{3,2,1,0:T(8,128)S(1)}, u32[]{:S(2)}, u32[]{:S(2)}) collective-permute-start(f32[2,2,16,512]{3,2,1,0:T(8,128)S(1)} %get-tuple-element.22), channel_id=1, source_target_pairs={{0,4},{1,5},{2,6},{3,7},{4,0},{5,1},{6,2},{7,3},{8,12},{9,13},{10,... | collective-permute-start | bytes 393224 | tf_op jit(solution)/shard_map/ppermute | solution.py:433
  80.3 20.8 %collective-permute-start.4 = (f32[2,2,16,512]{3,2,1,0:T(8,128)S(1)}, f32[2,2,16,512]{3,2,1,0:T(8,128)S(1)}, u32[]{:S(2)}, u32[]{:S(2)}) collective-permute-start(f32[2,2,16,512]{3,2,1,0:T(8,128)S(1)} %get-tuple-element.23), channel_id=1, source_target_pairs={{0,6},{1,7},{2,4},{3,5},{4,2},{5,3},{6,0},{7,1},{8,14},{9,15},{10,... | collective-permute-start | bytes 393224 | tf_op jit(solution)/shard_map/ppermute | solution.py:433
  101.2 21.4 %collective-permute-start.5 = (f32[4,2,16,512]{3,2,1,0:T(8,128)S(1)}, f32[4,2,16,512]{3,2,1,0:T(8,128)S(1)}, u32[]{:S(2)}, u32[]{:S(2)}) collective-permute-start(f32[4,2,16,512]{3,2,1,0:T(8,128)S(1)} %pad_maximum_fusion), channel_id=1, source_target_pairs={{0,1},{1,0},{2,3},{3,2},{4,5},{5,4},{6,7},{7,6},{8,9},{9,8},{10,11... | collective-permute-start | bytes 786440 | tf_op jit(solution)/shard_map/ppermute | solution.py:433

commit v3 on v2

--- a/solution.py
+++ b/solution.py
@@ -293,34 +293,58 @@
     return result[0], result[1:]
 
 
-def windows_kernel(own, halo, field, screen, above, below, out):
-    rows = screen.shape[0]
+def edges_kernel(halo, field, screen, held, top, bottom, arrived):
+    rows = held.shape[1]
+    copies = [
+        pltpu.make_async_copy(field, held.at[0:2], arrived.at[0]),
+        pltpu.make_async_copy(screen, held.at[2], arrived.at[1]),
+    ]
+    for copy in copies:
+        copy.start()
+    for copy in copies:
+        copy.wait()
+    top[...] = held[:, 0:halo]
+    bottom[...] = held[:, rows - halo : rows]
+
+
+def take_edges(field, screen, halo):
+    rows, cols = screen.shape
+    vmem = pl.BlockSpec(memory_space=pltpu.VMEM)
+    return pl.pallas_call(
+        lambda *refs: edges_kernel(halo, *refs),
+        out_shape=[jax.ShapeDtypeStruct((3, count, cols), jnp.float32) for count in (rows, halo, halo)],
+        in_specs=[IN_PLACE] * 2,
+        out_specs=[vmem] * 3,
+        scratch_shapes=[pltpu.SemaphoreType.DMA((2,))],
+        compiler_params=pltpu.CompilerParams(vmem_limit_bytes=4 * 1024 * 1024),
+        name="edges",
+    )(kept_out(field), kept_out(screen))
+
+
+def windows_kernel(own, halo, sector, above, below, out):
+    rows = sector.shape[1]
     for target in range(rows // own):
         first = target * own - halo
-        for row in range(first, first + own + 2 * halo, own):
-            to = slice(row - first, row - first + own)
-            for part in range(3):
-                if row < 0:
-                    out[target, part, to] = above[part]
-                elif row >= rows:
-                    out[target, part, to] = below[part]
-                elif part < 2:
-                    out[target, part, to] = field[part, row : row + own]
-                else:
-                    out[target, part, to] = screen[row : row + own]
-
-
-def make_windows(field, screen, above, below, own, halo):
-    rows, cols = screen.shape
+        low = max(first, 0)
+        high = min(first + own + 2 * halo, rows)
+        out[target, :, low - first : high - first] = sector[:, low:high]
+        if low > first:
+            out[target, :, : low - first] = above[...]
+        if high < first + own + 2 * halo:
+            out[target, :, high - first :] = below[...]
+
+
+def make_windows(sector, above, below, own, halo):
+    _, rows, cols = sector.shape
     vmem = pl.BlockSpec(memory_space=pltpu.VMEM)
     return pl.pallas_call(
         lambda *refs: windows_kernel(own, halo, *refs),
         out_shape=jax.ShapeDtypeStruct((rows // own, 3, own + 2 * halo, cols), jnp.float32),
-        in_specs=[vmem] * 4,
+        in_specs=[vmem] * 3,
         out_specs=vmem,
         compiler_params=pltpu.CompilerParams(vmem_limit_bytes=4 * 1024 * 1024),
         name="windows",
-    )(field, screen, above, below)
+    )(sector, above, below)
 
 
 def add_groups(total, term, marks):
@@ -444,15 +468,13 @@
     halo = 2 * steps
     blocks_here = cols_here // LABEL_BLOCK
 
-    def edge(rows):
-        return jnp.concatenate([adjoint_in[:, rows], screen[None, rows]])
-
+    sector, top, bottom = take_edges(adjoint_in, screen, halo)
     ahead = [(i, (i + 1) % sectors) for i in range(sectors)]
     behind = [((i + 1) % sectors, i) for i in range(sectors)]
-    above = lax.ppermute(edge(slice(rows_here - halo, rows_here)), "az", ahead)
-    below = lax.ppermute(edge(slice(0, halo)), "az", behind)
-
-    windows = make_windows(adjoint_in, screen, above, below, own, halo)
+    above = lax.ppermute(bottom, "az", ahead)
+    below = lax.ppermute(top, "az", behind)
+
+    windows = make_windows(sector, above, below, own, halo)
     window = lax.all_to_all(windows, "dep", 0, 0)
 
     weight = bed_weight.reshape(ranges, 1, cols_here)
@@ -473,7 +495,8 @@
     across = jnp.stack([pair[1] for pair in ready])
     field = gather_rows(rank, swap(across, 1, ranges), ready)
     sums = jnp.broadcast_to(sums[None, 0, :GROUPS], (sectors * ranges, GROUPS))
-    sums = jnp.sum(lax.all_to_all(sums, ("az", "dep"), 0, 0), axis=0)
+    sums, field = lax.optimization_barrier((lax.all_to_all(sums, ("az", "dep"), 0, 0), field))
+    sums = jnp.sum(sums, axis=0)
     return (field, sums)
 
 

time: 124 us -> 121 us (0.976)
  blocking collectives: 19.8 us -> 0 us
  starting transfers between devices: 17.8 us -> 28.2 us
  waiting for transfers between devices: 45.8 us -> 54.6 us
  local copies, waits for them, and re-layouts: 9.71 us -> 6.68 us
    all_to_all x1 -> x0, blocking collectives: 19.8 us -> none  [on_device(): sums = jnp.sum(lax.all_to_all(sums, ('az', 'dep'), 0, 0), axis=0)]
    all_to_all x0 -> x1, starting transfers between devices: none -> 10.6 us  [on_device(): lax.all_to_all(sums, ('az', 'dep'), 0, 0)]
    all_to_all x0 -> x1, waiting for transfers between devices: none -> 8.86 us  [on_device(): lax.all_to_all(sums, ('az', 'dep'), 0, 0)]
    unnamed x13 -> x9, local copies, waits for them, and re-layouts: 3.5 us -> 1.51 us
  transfers between devices with their start and end apart: 8 -> 9, of which waited for: 6 -> 7; matrix products, arithmetic and copies ran while one was open for 3% -> 3% of each run, Pallas kernels for 21% -> 23%
where the time goes in v3:
time: 121 us
  waiting for transfers between devices  54.6 us (45%)
  Pallas kernels  30 us (25%)
  starting transfers between devices  28.2 us (23%)
  local copies, waits for them, and re-layouts  6.68 us (6%)
    all_to_all x1, waiting for transfers between devices, on_device(): window = lax.all_to_all(windows, 'dep', 0, 0)  22.8 us
    pallas_call x1, Pallas kernels, run_steps(): pl.pallas_call(lambda *refs: steps_kernel(steps, halo, *refs), out_shape=...  22.7 us
    all_to_all x1, waiting for transfers between devices, on_device(): stored = lax.all_to_all(stored, 'dep', 0, 0)  16.2 us
    all_to_all x1, starting transfers between devices, on_device(): lax.all_to_all(sums, ('az', 'dep'), 0, 0)  10.6 us
    all_to_all x1, waiting for transfers between devices, on_device(): lax.all_to_all(sums, ('az', 'dep'), 0, 0)  8.86 us
    ppermute x4, starting transfers between devices, swap(): return lax.ppermute(value, 'dep', [(i, i ^ other) for i in range(count)])  4.72 us
    all_to_all x1, starting transfers between devices, on_device(): stored = lax.all_to_all(stored, 'dep', 0, 0)  4.49 us
    all_to_all x1, starting transfers between devices, on_device(): window = lax.all_to_all(windows, 'dep', 0, 0)  4.22 us
  transfers between devices with their start and end apart: 9, of which 7 were waited for; matrix products, arithmetic and copies ran while one was open for 3% of the time, Pallas kernels for 23%

profile of v3, /device:TPU:1, one launch (start us, length us, event | category | flops | bytes accessed | tf_op | source)
XLA Modules:
  0.0 120.8 jit_solution(6877661743798952234)
XLA Ops:
  0.6 0.0 copy-start
  0.6 1.1 edges.1
  1.8 4.2 %collective-permute-start = (f32[3,16,512]{2,1,0:T(8,128)S(1)}, f32[3,16,512]{2,1,0:T(8,128)S(1)}, u32[]{:S(2)}, u32[]{:S(2)}) collective-permute-start(f32[3,16,512]{2,1,0:T(8,128)S(1)} %get-tuple-element.21), channel_id=1, source_target_pairs={{0,8},{8,16},{16,24},{24,32},{32,40},{40,48},{48,56},{56,64},{64,7... | collective-permute-start | bytes 294920 | tf_op jit(solution)/shard_map/ppermute | solution.py:474
  6.0 0.0 collective-permute-start.1
  6.0 1.6 %collective-permute-done.refs_1_ = f32[3,16,512]{2,1,0:T(8,128)S(1)} collective-permute-done((f32[3,16,512]{2,1,0:T(8,128)S(1)}, f32[3,16,512]{2,1,0:T(8,128)S(1)}, u32[]{:S(2)}, u32[]{:S(2)}) %collective-permute-start) | collective-permute-done | bytes 98336 | tf_op jit(solution)/shard_map/ppermute | solution.py:474
  7.6 3.9 %collective-permute-done.1.refs_2_ = f32[3,16,512]{2,1,0:T(8,128)S(1)} collective-permute-done((f32[3,16,512]{2,1,0:T(8,128)S(1)}, f32[3,16,512]{2,1,0:T(8,128)S(1)}, u32[]{:S(2)}, u32[]{:S(2)}) %collective-permute-start.1) | collective-permute-done | bytes 98336 | tf_op jit(solution)/shard_map/ppermute | solution.py:475
  11.5 1.6 %windows.1 = f32[8,3,48,512]{3,2,1,0:T(8,128)} custom-call(f32[3,128,512]{2,1,0:T(8,128)S(1)} %get-tuple-element.20.refs_0_, f32[3,16,512]{2,1,0:T(8,128)S(1)} %collective-permute-done.refs_1_, f32[3,16,512]{2,1,0:T(8,128)S(1)} %collective-permute-done.1.refs_2_), custom_call_target="tpu_custom_call" | custom-call | tf_op jit(solution)/shard_map/windows/pallas_call | solution.py:340
  13.1 4.2 %all-to-all-start = ((f32[8,3,48,512]{3,2,1,0:T(8,128)}), f32[8,3,48,512]{3,2,1,0:T(8,128)S(1)}, u32[]{:S(2)}, u32[]{:S(2)}) async-start(f32[8,3,48,512]{3,2,1,0:T(8,128)} %windows.1), calls=%async_computation | async-start | bytes 4718592 | tf_op jit(solution)/shard_map/all_to_all | solution.py:478
  17.3 0.0 copy-done
  17.3 0.1 constant_dynamic-slice_fusion
  17.4 0.1 copy.12
  17.5 0.1 copy.14.marks
  17.7 0.0 slice-start
  17.7 2.0 %slice-done = f32[7,2,128,512]{3,2,1,0:T(8,128)S(1)} async-done(((f32[8,2,128,512]{3,2,1,0:T(8,128)}), f32[7,2,128,512]{3,2,1,0:T(8,128)S(1)}, s32[]{:S(2)}) %slice-start) | async-done | bytes 3670040 | tf_op jit(solution)/shard_map/slice | solution.py:486
  19.7 0.0 copy-start.1
  19.7 0.0 copy-start.2
  19.7 0.0 copy-start.3
  19.7 2.2 %copy.16 = f32[7,2,8,16,512]{4,3,1,0,2:T(8,128)} copy(f32[7,2,8,16,512]{4,3,2,1,0:T(8,128)S(1)} %bitcast.11) | data formatting | bytes 7340032 | tf_op jit(solution)/shard_map/reshape | solution.py:486
  21.9 1.3 %copy-done.1 = f32[8,2,128,512]{3,2,1,0:T(8,128)S(1)} copy-done((f32[8,2,128,512]{3,2,1,0:T(8,128)S(1)}, f32[8,2,128,512]{3,2,1,0:T(8,128)}, u32[]{:S(2)}) %copy-start.1) | copy-done | bytes 4194328
  23.2 0.1 copy-done.2
  23.3 0.0 copy-done.3
  23.3 0.4 here.1
  23.7 22.8 %all-to-all-done.refs_1_ = f32[8,3,48,512]{3,2,1,0:T(8,128)S(1)} async-done(((f32[8,3,48,512]{3,2,1,0:T(8,128)}), f32[8,3,48,512]{3,2,1,0:T(8,128)S(1)}, u32[]{:S(2)}, u32[]{:S(2)}) %all-to-all-start) | async-done | bytes 2359328 | tf_op jit(solution)/shard_map/all_to_all | solution.py:478
  46.5 4.5 %all-to-all-start.1 = ((f32[8,7,2,16,512]{4,3,2,1,0:T(8,128)}), f32[8,7,2,16,512]{4,3,2,1,0:T(8,128)}, u32[]{:S(2)}, u32[]{:S(2)}) async-start(f32[8,7,2,16,512]{4,3,2,1,0:T(8,128)} %bitcast.15), calls=%async_computation.1 | async-start | bytes 7340032 | tf_op jit(solution)/shard_map/all_to_all | solution.py:489
  51.0 22.7 %steps.1 = (f32[7,8,2,16,512]{4,3,2,1,0:T(8,128)}, f32[2,2,16,512]{3,2,1,0:T(8,128)S(1)}, f32[2,2,16,512]{3,2,1,0:T(8,128)S(1)}, f32[2,2,16,512]{3,2,1,0:T(8,128)S(1)}, f32[2,2,16,512]{3,2,1,0:T(8,128)S(1)}) custom-call(s32[1]{0:T(128)} %bitcast.rank.refs_0_, f32[8,3,48,512]{3,2,1,0:T(8,128)S(1)} %all-to-all-done.refs_1_, ...), custom_call_target="tpu_custom_call" | custom-call | flops 20000000000 | bytes 8000000 | tf_op jit(solution)/shard_map/steps/pallas_call | solution.py:268
  73.8 1.4 %collective-permute-start.2 = (f32[2,2,16,512]{3,2,1,0:T(8,128)S(1)}, f32[2,2,16,512]{3,2,1,0:T(8,128)S(1)}, u32[]{:S(2)}, u32[]{:S(2)}) collective-permute-start(f32[2,2,16,512]{3,2,1,0:T(8,128)S(1)} %get-tuple-element.29), channel_id=1, source_target_pairs={{0,2},{1,3},{2,0},{3,1},{4,6},{5,7},{6,4},{7,5},{8,10},{9,11},{10,... | collective-permute-start | bytes 393224 | tf_op jit(solution)/shard_map/ppermute | solution.py:457
  75.2 2.4 %collective-permute-start.3 = (f32[2,2,16,512]{3,2,1,0:T(8,128)S(1)}, f32[2,2,16,512]{3,2,1,0:T(8,128)S(1)}, u32[]{:S(2)}, u32[]{:S(2)}) collective-permute-start(f32[2,2,16,512]{3,2,1,0:T(8,128)S(1)} %get-tuple-element.30), channel_id=1, source_target_pairs={{0,4},{1,5},{2,6},{3,7},{4,0},{5,1},{6,2},{7,3},{8,12},{9,13},{10,... | collective-permute-start | bytes 393224 | tf_op jit(solution)/shard_map/ppermute | solution.py:457
  77.6 0.1 collective-permute-start.4
  77.7 16.2 %all-to-all-done.1.stored_at = f32[8,7,2,16,512]{4,3,2,1,0:T(8,128)} async-done(((f32[8,7,2,16,512]{4,3,2,1,0:T(8,128)}), f32[8,7,2,16,512]{4,3,2,1,0:T(8,128)}, u32[]{:S(2)}, u32[]{:S(2)}) %all-to-all-start.1) | async-done | bytes 3670048 | tf_op jit(solution)/shard_map/all_to_all | solution.py:489
  93.9 3.4 %sums.1 = f32[1,128]{1,0:T(1,128)S(1)} custom-call(f32[7,8,2,16,512]{4,3,2,1,0:T(8,128)} %get-tuple-element.24.past_at, f32[8,7,2,16,512]{4,3,2,1,0:T(8,128)} %all-to-all-done.1.stored_at, f32[8,1,512]{2,1,0:T(1,128)S(1)} %bitcast.14, s32[8,16,4]{2,1,0:T(8,128)S(1)} %bitcast.12, f32[8,128]{1,0:T(8,128)S(1)} %here.1), custom_call_target="tpu_custom_call" | custom-call | tf_op jit(solution)/shard_map/sums/pallas_call | solution.py:419
  97.3 0.0 collective-permute-done.2.refs_1_
  97.3 0.6 collective-permute-done.3.refs_2_
  97.9 0.5 collective-permute-done.4.refs_3_
  98.5 0.8 collective-permute-start.5
  99.3 0.7 broadcast_in_dim.2
  100.0 10.6 %all-to-all-start.2 = ((f32[128,1,32]{2,1,0:T(1,128)}), f32[128,1,32]{2,1,0:T(1,128)S(1)}, u32[]{:S(2)}, u32[]{:S(2)}) async-start(f32[128,1,32]{2,1,0:T(1,128)} %broadcast_in_dim.2), calls=%async_computation.2 | async-start | bytes 131072 | tf_op jit(solution)/shard_map/all_to_all | solution.py:498
  110.5 0.0 collective-permute-done.5.across
  110.5 0.8 gather.1
  111.4 8.9 %all-to-all-done.2 = f32[128,1,32]{2,1,0:T(1,128)S(1)} async-done(((f32[128,1,32]{2,1,0:T(1,128)}), f32[128,1,32]{2,1,0:T(1,128)S(1)}, u32[]{:S(2)}, u32[]{:S(2)}) %all-to-all-start.2) | async-done | bytes 16416 | tf_op jit(solution)/shard_map/all_to_all | solution.py:498
  120.2 0.5 reduce_sum.9
  (7 shorter events, 0.1 us)
Async XLA Ops:
  0.6 16.7 %copy-start = (s32[128,32]{0,1:T(8,128)S(1)}, s32[128,32]{0,1:T(8,128)}, u32[]{:S(2)}) copy-start(s32[128,32]{0,1:T(8,128)} %param.12) | copy-start | bytes 49156
  1.8 5.8 %collective-permute-start = (f32[3,16,512]{2,1,0:T(8,128)S(1)}, f32[3,16,512]{2,1,0:T(8,128)S(1)}, u32[]{:S(2)}, u32[]{:S(2)}) collective-permute-start(f32[3,16,512]{2,1,0:T(8,128)S(1)} %get-tuple-element.21), channel_id=1, source_target_pairs={{0,8},{8,16},{16,24},{24,32},{32,40},{40,48},{48,56},{56,64},{64,7... | collective-permute-start | bytes 294920 | tf_op jit(solution)/shard_map/ppermute | solution.py:474
  6.0 5.5 %collective-permute-start.1 = (f32[3,16,512]{2,1,0:T(8,128)S(1)}, f32[3,16,512]{2,1,0:T(8,128)S(1)}, u32[]{:S(2)}, u32[]{:S(2)}) collective-permute-start(f32[3,16,512]{2,1,0:T(8,128)S(1)} %get-tuple-element.22), channel_id=1, source_target_pairs={{8,0},{16,8},{24,16},{32,24},{40,32},{48,40},{56,48},{64,56},{72,6... | collective-permute-start | bytes 294920 | tf_op jit(solution)/shard_map/ppermute | solution.py:475
  13.1 33.4 %all-to-all-start = ((f32[8,3,48,512]{3,2,1,0:T(8,128)}), f32[8,3,48,512]{3,2,1,0:T(8,128)S(1)}, u32[]{:S(2)}, u32[]{:S(2)}) async-start(f32[8,3,48,512]{3,2,1,0:T(8,128)} %windows.1), calls=%async_computation | async-start | bytes 4718592 | tf_op jit(solution)/shard_map/all_to_all | solution.py:478
  17.7 2.0 %slice-start = ((f32[8,2,128,512]{3,2,1,0:T(8,128)}), f32[7,2,128,512]{3,2,1,0:T(8,128)S(1)}, s32[]{:S(2)}) async-start(f32[8,2,128,512]{3,2,1,0:T(8,128)} %latest.1), calls=%async_computation.3 | async-start | bytes 7340032 | tf_op jit(solution)/shard_map/slice | solution.py:486
  19.7 3.5 %copy-start.1 = (f32[8,2,128,512]{3,2,1,0:T(8,128)S(1)}, f32[8,2,128,512]{3,2,1,0:T(8,128)}, u32[]{:S(2)}) copy-start(f32[8,2,128,512]{3,2,1,0:T(8,128)} %latest.1) | copy-start | bytes 12582916
  19.7 3.6 %copy-start.2 = (f32[2,128,512]{2,1,0:T(8,128)S(1)}, f32[2,128,512]{2,1,0:T(8,128)}, u32[]{:S(2)}) copy-start(f32[2,128,512]{2,1,0:T(8,128)} %field.1) | copy-start | bytes 1572868
  19.7 3.6 %copy-start.3 = (f32[4096]{0:T(1024)S(1)}, f32[4096]{0:T(1024)}, u32[]{:S(2)}) copy-start(f32[4096]{0:T(1024)} %param.11) | copy-start | bytes 49156
  46.5 47.4 %all-to-all-start.1 = ((f32[8,7,2,16,512]{4,3,2,1,0:T(8,128)}), f32[8,7,2,16,512]{4,3,2,1,0:T(8,128)}, u32[]{:S(2)}, u32[]{:S(2)}) async-start(f32[8,7,2,16,512]{4,3,2,1,0:T(8,128)} %bitcast.15), calls=%async_computation.1 | async-start | bytes 7340032 | tf_op jit(solution)/shard_map/all_to_all | solution.py:489
  73.8 23.6 %collective-permute-start.2 = (f32[2,2,16,512]{3,2,1,0:T(8,128)S(1)}, f32[2,2,16,512]{3,2,1,0:T(8,128)S(1)}, u32[]{:S(2)}, u32[]{:S(2)}) collective-permute-start(f32[2,2,16,512]{3,2,1,0:T(8,128)S(1)} %get-tuple-element.29), channel_id=1, source_target_pairs={{0,2},{1,3},{2,0},{3,1},{4,6},{5,7},{6,4},{7,5},{8,10},{9,11},{10,... | collective-permute-start | bytes 393224 | tf_op jit(solution)/shard_map/ppermute | solution.py:457
  75.2 22.7 %collective-permute-start.3 = (f32[2,2,16,512]{3,2,1,0:T(8,128)S(1)}, f32[2,2,16,512]{3,2,1,0:T(8,128)S(1)}, u32[]{:S(2)}, u32[]{:S(2)}) collective-permute-start(f32[2,2,16,512]{3,2,1,0:T(8,128)S(1)} %get-tuple-element.30), channel_id=1, source_target_pairs={{0,4},{1,5},{2,6},{3,7},{4,0},{5,1},{6,2},{7,3},{8,12},{9,13},{10,... | collective-permute-start | bytes 393224 | tf_op jit(solution)/shard_map/ppermute | solution.py:457
  77.6 20.8 %collective-permute-start.4 = (f32[2,2,16,512]{3,2,1,0:T(8,128)S(1)}, f32[2,2,16,512]{3,2,1,0:T(8,128)S(1)}, u32[]{:S(2)}, u32[]{:S(2)}) collective-permute-start(f32[2,2,16,512]{3,2,1,0:T(8,128)S(1)} %get-tuple-element.31), channel_id=1, source_target_pairs={{0,6},{1,7},{2,4},{3,5},{4,2},{5,3},{6,0},{7,1},{8,14},{9,15},{10,... | collective-permute-start | bytes 393224 | tf_op jit(solution)/shard_map/ppermute | solution.py:457
  98.5 12.0 %collective-permute-start.5 = (f32[4,2,16,512]{3,2,1,0:T(8,128)S(1)}, f32[4,2,16,512]{3,2,1,0:T(8,128)S(1)}, u32[]{:S(2)}, u32[]{:S(2)}) collective-permute-start(f32[4,2,16,512]{3,2,1,0:T(8,128)S(1)} %pad_maximum_fusion), channel_id=1, source_target_pairs={{0,1},{1,0},{2,3},{3,2},{4,5},{5,4},{6,7},{7,6},{8,9},{9,8},{10,11... | collective-permute-start | bytes 786440 | tf_op jit(solution)/shard_map/ppermute | solution.py:457
  100.0 20.3 %all-to-all-start.2 = ((f32[128,1,32]{2,1,0:T(1,128)}), f32[128,1,32]{2,1,0:T(1,128)S(1)}, u32[]{:S(2)}, u32[]{:S(2)}) async-start(f32[128,1,32]{2,1,0:T(1,128)} %broadcast_in_dim.2), calls=%async_computation.2 | async-start | bytes 131072 | tf_op jit(solution)/shard_map/all_to_all | solution.py:498

commit v4 on v3

--- a/solution.py
+++ b/solution.py
@@ -227,7 +227,7 @@
                         turn_screen(turned[p], p, q, base)
 
     def leave(at):
-        return pltpu.make_async_copy(past.at[at], past_at.at[at], left.at[at])
+        return pltpu.make_async_copy(past.at[at], past_at.at[:, at], left.at[at])
 
     spans = []
     for index in range(steps):
@@ -267,7 +267,7 @@
     field = (sources, inner)
     result = pl.pallas_call(
         lambda *refs: steps_kernel(steps, halo, *refs),
-        out_shape=[pltpu.HBM((steps - 1, sources, 2, own, cols), jnp.float32)]
+        out_shape=[pltpu.HBM((sources, steps - 1, 2, own, cols), jnp.float32)]
         + [jax.ShapeDtypeStruct((2, 2, own, cols), jnp.float32)] * (sources // 2),
         in_specs=[SCALARS, vmem] + [IN_PLACE] * 3,
         out_specs=[IN_PLACE] + [vmem] * (sources // 2),
@@ -386,13 +386,13 @@
 
 
 def sums_kernel(past_at, stored_at, weight, marks, here, out, past, stored, arrived):
-    steps, sources, _, own, _ = past.shape
+    sources, steps, _, own, _ = past.shape
     copies = []
     for source in range(sources):
         copies.append(
             (
                 pltpu.make_async_copy(stored_at.at[source], stored.at[source], arrived.at[0, source]),
-                pltpu.make_async_copy(past_at.at[:, source], past.at[:, source], arrived.at[1, source]),
+                pltpu.make_async_copy(past_at.at[source], past.at[source], arrived.at[1, source]),
             )
         )
     for pair in copies:
@@ -407,24 +407,24 @@
             term = None
             for index in range(steps):
                 kept = steps - 1 - index
-                one = past[index, source, 1, at] * stored[source, kept, 0, at]
-                two = past[index, source, 0, at] * stored[source, kept, 1, at]
+                one = past[source, index, 1, at] * stored[source, kept, 0, at]
+                two = past[source, index, 0, at] * stored[source, kept, 1, at]
                 term = one - two if term is None else term + (one - two)
             total = add_groups(total, term * weight[source], marks[source, at])
-    out[...] = jnp.sum(total, axis=0, keepdims=True)
-
-
-def group_sums(past, stored, weight, marks, here):
+    out[...] = jnp.broadcast_to(jnp.sum(total, axis=0, keepdims=True)[None], out.shape)
+
+
+def group_sums(past, stored, weight, marks, here, devices):
     vmem = pl.BlockSpec(memory_space=pltpu.VMEM)
     return pl.pallas_call(
         sums_kernel,
-        out_shape=jax.ShapeDtypeStruct((1, LANES), jnp.float32),
+        out_shape=jax.ShapeDtypeStruct((devices, 1, LANES), jnp.float32),
         in_specs=[IN_PLACE] * 2 + [vmem] * 3,
         out_specs=vmem,
         scratch_shapes=[
             pltpu.VMEM(past.shape, jnp.float32),
             pltpu.VMEM(stored.shape, jnp.float32),
-            pltpu.SemaphoreType.DMA((2, past.shape[1])),
+            pltpu.SemaphoreType.DMA((2, past.shape[0])),
         ],
         compiler_params=pltpu.CompilerParams(vmem_limit_bytes=10 * 1024 * 1024),
         name="sums",
@@ -490,13 +490,12 @@
 
     past, pairs = run_steps(window, rank, steps, halo)
     pairs = [pairs[0]] + [swap(pairs[number], 2 * number, ranges) for number in range(1, ranges // 2)]
-    sums = group_sums(past, stored, weight, marks, here)
+    sums = group_sums(past, stored, weight, marks, here, sectors * ranges)
     _, *ready = lax.optimization_barrier((sums, *pairs))
     across = jnp.stack([pair[1] for pair in ready])
     field = gather_rows(rank, swap(across, 1, ranges), ready)
-    sums = jnp.broadcast_to(sums[None, 0, :GROUPS], (sectors * ranges, GROUPS))
     sums, field = lax.optimization_barrier((lax.all_to_all(sums, ("az", "dep"), 0, 0), field))
-    sums = jnp.sum(sums, axis=0)
+    sums = jnp.sum(sums, axis=(0, 1))[:GROUPS]
     return (field, sums)
 
 

time: 121 us -> 121 us (level)
  transfers between devices with their start and end apart: 9 -> 9, of which waited for: 7 -> 6; matrix products, arithmetic and copies ran while one was open for 3% -> 2% of each run, Pallas kernels for 23% -> 23%
where the time goes in v4:
time: 121 us; the launch traced here: 120 us
  waiting for transfers between devices  53.9 us (45%)
  Pallas kernels  30.7 us (25%)
  starting transfers between devices  28.2 us (23%)
  local copies, waits for them, and re-layouts  6.01 us (5%)
    all_to_all x1, waiting for transfers between devices, on_device(): window = lax.all_to_all(windows, 'dep', 0, 0)  22.8 us
    pallas_call x1, Pallas kernels, run_steps(): pl.pallas_call(lambda *refs: steps_kernel(steps, halo, *refs), out_shape=...  22.7 us
    all_to_all x1, waiting for transfers between devices, on_device(): stored = lax.all_to_all(stored, 'dep', 0, 0)  16.2 us
    all_to_all x1, starting transfers between devices, on_device(): lax.all_to_all(sums, ('az', 'dep'), 0, 0)  10.6 us
    all_to_all x1, waiting for transfers between devices, on_device(): lax.all_to_all(sums, ('az', 'dep'), 0, 0)  8.86 us
    ppermute x4, starting transfers between devices, swap(): return lax.ppermute(value, 'dep', [(i, i ^ other) for i in range(count)])  4.72 us
    all_to_all x1, starting transfers between devices, on_device(): stored = lax.all_to_all(stored, 'dep', 0, 0)  4.5 us
    all_to_all x1, starting transfers between devices, on_device(): window = lax.all_to_all(windows, 'dep', 0, 0)  4.22 us
  transfers between devices with their start and end apart: 9, of which 6 were waited for; matrix products, arithmetic and copies ran while one was open for 2% of the time, Pallas kernels for 23%

profile of v4, /device:TPU:1, one launch (start us, length us, event | category | flops | bytes accessed | tf_op | source)
XLA Modules:
  0.0 120.3 jit_solution(3900677642424559096)
XLA Ops:
  0.6 0.0 copy-start
  0.6 1.1 edges.1
  1.8 4.2 %collective-permute-start = (f32[3,16,512]{2,1,0:T(8,128)S(1)}, f32[3,16,512]{2,1,0:T(8,128)S(1)}, u32[]{:S(2)}, u32[]{:S(2)}) collective-permute-start(f32[3,16,512]{2,1,0:T(8,128)S(1)} %get-tuple-element.21), channel_id=1, source_target_pairs={{0,8},{8,16},{16,24},{24,32},{32,40},{40,48},{48,56},{56,64},{64,7... | collective-permute-start | bytes 294920 | tf_op jit(solution)/shard_map/ppermute | solution.py:474
  6.0 0.0 collective-permute-start.1
  6.0 1.6 %collective-permute-done.refs_1_ = f32[3,16,512]{2,1,0:T(8,128)S(1)} collective-permute-done((f32[3,16,512]{2,1,0:T(8,128)S(1)}, f32[3,16,512]{2,1,0:T(8,128)S(1)}, u32[]{:S(2)}, u32[]{:S(2)}) %collective-permute-start) | collective-permute-done | bytes 98336 | tf_op jit(solution)/shard_map/ppermute | solution.py:474
  7.6 3.9 %collective-permute-done.1.refs_2_ = f32[3,16,512]{2,1,0:T(8,128)S(1)} collective-permute-done((f32[3,16,512]{2,1,0:T(8,128)S(1)}, f32[3,16,512]{2,1,0:T(8,128)S(1)}, u32[]{:S(2)}, u32[]{:S(2)}) %collective-permute-start.1) | collective-permute-done | bytes 98336 | tf_op jit(solution)/shard_map/ppermute | solution.py:475
  11.5 1.6 %windows.1 = f32[8,3,48,512]{3,2,1,0:T(8,128)} custom-call(f32[3,128,512]{2,1,0:T(8,128)S(1)} %get-tuple-element.20.refs_0_, f32[3,16,512]{2,1,0:T(8,128)S(1)} %collective-permute-done.refs_1_, f32[3,16,512]{2,1,0:T(8,128)S(1)} %collective-permute-done.1.refs_2_), custom_call_target="tpu_custom_call" | custom-call | tf_op jit(solution)/shard_map/windows/pallas_call | solution.py:340
  13.1 4.2 %all-to-all-start = ((f32[8,3,48,512]{3,2,1,0:T(8,128)}), f32[8,3,48,512]{3,2,1,0:T(8,128)S(1)}, u32[]{:S(2)}, u32[]{:S(2)}) async-start(f32[8,3,48,512]{3,2,1,0:T(8,128)} %windows.1), calls=%async_computation | async-start | bytes 4718592 | tf_op jit(solution)/shard_map/all_to_all | solution.py:478
  17.4 0.0 copy-done
  17.4 0.1 constant_dynamic-slice_fusion
  17.4 0.1 copy.12
  17.6 0.1 copy.14.marks
  17.7 0.0 slice-start
  17.7 2.0 %slice-done = f32[7,2,128,512]{3,2,1,0:T(8,128)S(1)} async-done(((f32[8,2,128,512]{3,2,1,0:T(8,128)}), f32[7,2,128,512]{3,2,1,0:T(8,128)S(1)}, s32[]{:S(2)}) %slice-start) | async-done | bytes 3670040 | tf_op jit(solution)/shard_map/slice | solution.py:486
  19.7 0.0 copy-start.1
  19.7 0.0 copy-start.2
  19.7 0.0 copy-start.3
  19.7 2.3 %copy.16 = f32[7,2,8,16,512]{4,3,1,0,2:T(8,128)} copy(f32[7,2,8,16,512]{4,3,2,1,0:T(8,128)S(1)} %bitcast.9) | data formatting | bytes 7340032 | tf_op jit(solution)/shard_map/reshape | solution.py:486
  22.0 1.2 %copy-done.1 = f32[8,2,128,512]{3,2,1,0:T(8,128)S(1)} copy-done((f32[8,2,128,512]{3,2,1,0:T(8,128)S(1)}, f32[8,2,128,512]{3,2,1,0:T(8,128)}, u32[]{:S(2)}) %copy-start.1) | copy-done | bytes 4194328
  23.2 0.1 copy-done.2
  23.4 0.0 copy-done.3
  23.4 0.4 here.1
  23.7 22.8 %all-to-all-done.refs_1_ = f32[8,3,48,512]{3,2,1,0:T(8,128)S(1)} async-done(((f32[8,3,48,512]{3,2,1,0:T(8,128)}), f32[8,3,48,512]{3,2,1,0:T(8,128)S(1)}, u32[]{:S(2)}, u32[]{:S(2)}) %all-to-all-start) | async-done | bytes 2359328 | tf_op jit(solution)/shard_map/all_to_all | solution.py:478
  46.6 4.5 %all-to-all-start.1 = ((f32[8,7,2,16,512]{4,3,2,1,0:T(8,128)}), f32[8,7,2,16,512]{4,3,2,1,0:T(8,128)}, u32[]{:S(2)}, u32[]{:S(2)}) async-start(f32[8,7,2,16,512]{4,3,2,1,0:T(8,128)} %bitcast.13), calls=%async_computation.1 | async-start | bytes 7340032 | tf_op jit(solution)/shard_map/all_to_all | solution.py:489
  51.1 22.7 %steps.1 = (f32[8,7,2,16,512]{4,3,2,1,0:T(8,128)}, f32[2,2,16,512]{3,2,1,0:T(8,128)S(1)}, f32[2,2,16,512]{3,2,1,0:T(8,128)S(1)}, f32[2,2,16,512]{3,2,1,0:T(8,128)S(1)}, f32[2,2,16,512]{3,2,1,0:T(8,128)S(1)}) custom-call(s32[1]{0:T(128)} %bitcast.rank.refs_0_, f32[8,3,48,512]{3,2,1,0:T(8,128)S(1)} %all-to-all-done.refs_1_, ...), custom_call_target="tpu_custom_call" | custom-call | flops 20000000000 | bytes 8000000 | tf_op jit(solution)/shard_map/steps/pallas_call | solution.py:268
  73.8 1.4 %collective-permute-start.2 = (f32[2,2,16,512]{3,2,1,0:T(8,128)S(1)}, f32[2,2,16,512]{3,2,1,0:T(8,128)S(1)}, u32[]{:S(2)}, u32[]{:S(2)}) collective-permute-start(f32[2,2,16,512]{3,2,1,0:T(8,128)S(1)} %get-tuple-element.29), channel_id=1, source_target_pairs={{0,2},{1,3},{2,0},{3,1},{4,6},{5,7},{6,4},{7,5},{8,10},{9,11},{10,... | collective-permute-start | bytes 393224 | tf_op jit(solution)/shard_map/ppermute | solution.py:457
  75.2 2.4 %collective-permute-start.3 = (f32[2,2,16,512]{3,2,1,0:T(8,128)S(1)}, f32[2,2,16,512]{3,2,1,0:T(8,128)S(1)}, u32[]{:S(2)}, u32[]{:S(2)}) collective-permute-start(f32[2,2,16,512]{3,2,1,0:T(8,128)S(1)} %get-tuple-element.30), channel_id=1, source_target_pairs={{0,4},{1,5},{2,6},{3,7},{4,0},{5,1},{6,2},{7,3},{8,12},{9,13},{10,... | collective-permute-start | bytes 393224 | tf_op jit(solution)/shard_map/ppermute | solution.py:457
  77.6 0.1 collective-permute-start.4
  77.7 16.2 %all-to-all-done.1.stored_at = f32[8,7,2,16,512]{4,3,2,1,0:T(8,128)} async-done(((f32[8,7,2,16,512]{4,3,2,1,0:T(8,128)}), f32[8,7,2,16,512]{4,3,2,1,0:T(8,128)}, u32[]{:S(2)}, u32[]{:S(2)}) %all-to-all-start.1) | async-done | bytes 3670048 | tf_op jit(solution)/shard_map/all_to_all | solution.py:489
  94.0 4.0 %sums.1 = f32[128,1,128]{2,1,0:T(1,128)} custom-call(f32[8,7,2,16,512]{4,3,2,1,0:T(8,128)} %get-tuple-element.24.past_at, f32[8,7,2,16,512]{4,3,2,1,0:T(8,128)} %all-to-all-done.1.stored_at, f32[8,1,512]{2,1,0:T(1,128)S(1)} %bitcast.12, s32[8,16,4]{2,1,0:T(8,128)S(1)} %bitcast.10, f32[8,128]{1,0:T(8,128)S(1)} %here.1), custom_call_target="tpu_custom_call" | custom-call | tf_op jit(solution)/shard_map/sums/pallas_call | solution.py:419
  98.0 0.0 collective-permute-done.2.refs_1_
  98.0 0.0 collective-permute-done.3.refs_2_
  98.0 0.4 collective-permute-done.4.refs_3_
  98.5 0.8 collective-permute-start.5
  99.3 10.6 %all-to-all-start.2 = ((f32[128,1,128]{2,1,0:T(1,128)}), f32[128,1,128]{2,1,0:T(1,128)S(1)}, u32[]{:S(2)}, u32[]{:S(2)}) async-start(f32[128,1,128]{2,1,0:T(1,128)} %sums.1), calls=%async_computation.2 | async-start | bytes 131072 | tf_op jit(solution)/shard_map/all_to_all | solution.py:497
  109.9 0.0 collective-permute-done.5.across
  109.9 0.8 gather.1
  110.7 8.9 %all-to-all-done.2 = f32[128,1,128]{2,1,0:T(1,128)S(1)} async-done(((f32[128,1,128]{2,1,0:T(1,128)}), f32[128,1,128]{2,1,0:T(1,128)S(1)}, u32[]{:S(2)}, u32[]{:S(2)}) %all-to-all-start.2) | async-done | bytes 65568 | tf_op jit(solution)/shard_map/all_to_all | solution.py:497
  119.6 0.7 reduce_sum.9
  (6 shorter events, 0.0 us)
Async XLA Ops:
  0.6 16.7 %copy-start = (s32[128,32]{0,1:T(8,128)S(1)}, s32[128,32]{0,1:T(8,128)}, u32[]{:S(2)}) copy-start(s32[128,32]{0,1:T(8,128)} %param.12) | copy-start | bytes 49156
  1.8 5.8 %collective-permute-start = (f32[3,16,512]{2,1,0:T(8,128)S(1)}, f32[3,16,512]{2,1,0:T(8,128)S(1)}, u32[]{:S(2)}, u32[]{:S(2)}) collective-permute-start(f32[3,16,512]{2,1,0:T(8,128)S(1)} %get-tuple-element.21), channel_id=1, source_target_pairs={{0,8},{8,16},{16,24},{24,32},{32,40},{40,48},{48,56},{56,64},{64,7... | collective-permute-start | bytes 294920 | tf_op jit(solution)/shard_map/ppermute | solution.py:474
  6.0 5.5 %collective-permute-start.1 = (f32[3,16,512]{2,1,0:T(8,128)S(1)}, f32[3,16,512]{2,1,0:T(8,128)S(1)}, u32[]{:S(2)}, u32[]{:S(2)}) collective-permute-start(f32[3,16,512]{2,1,0:T(8,128)S(1)} %get-tuple-element.22), channel_id=1, source_target_pairs={{8,0},{16,8},{24,16},{32,24},{40,32},{48,40},{56,48},{64,56},{72,6... | collective-permute-start | bytes 294920 | tf_op jit(solution)/shard_map/ppermute | solution.py:475
  13.1 33.4 %all-to-all-start = ((f32[8,3,48,512]{3,2,1,0:T(8,128)}), f32[8,3,48,512]{3,2,1,0:T(8,128)S(1)}, u32[]{:S(2)}, u32[]{:S(2)}) async-start(f32[8,3,48,512]{3,2,1,0:T(8,128)} %windows.1), calls=%async_computation | async-start | bytes 4718592 | tf_op jit(solution)/shard_map/all_to_all | solution.py:478
  17.7 2.0 %slice-start = ((f32[8,2,128,512]{3,2,1,0:T(8,128)}), f32[7,2,128,512]{3,2,1,0:T(8,128)S(1)}, s32[]{:S(2)}) async-start(f32[8,2,128,512]{3,2,1,0:T(8,128)} %latest.1), calls=%async_computation.3 | async-start | bytes 7340032 | tf_op jit(solution)/shard_map/slice | solution.py:486
  19.7 3.5 %copy-start.1 = (f32[8,2,128,512]{3,2,1,0:T(8,128)S(1)}, f32[8,2,128,512]{3,2,1,0:T(8,128)}, u32[]{:S(2)}) copy-start(f32[8,2,128,512]{3,2,1,0:T(8,128)} %latest.1) | copy-start | bytes 12582916
  19.7 3.6 %copy-start.2 = (f32[2,128,512]{2,1,0:T(8,128)S(1)}, f32[2,128,512]{2,1,0:T(8,128)}, u32[]{:S(2)}) copy-start(f32[2,128,512]{2,1,0:T(8,128)} %field.1) | copy-start | bytes 1572868
  19.7 3.6 %copy-start.3 = (f32[4096]{0:T(1024)S(1)}, f32[4096]{0:T(1024)}, u32[]{:S(2)}) copy-start(f32[4096]{0:T(1024)} %param.11) | copy-start | bytes 49156
  46.6 47.4 %all-to-all-start.1 = ((f32[8,7,2,16,512]{4,3,2,1,0:T(8,128)}), f32[8,7,2,16,512]{4,3,2,1,0:T(8,128)}, u32[]{:S(2)}, u32[]{:S(2)}) async-start(f32[8,7,2,16,512]{4,3,2,1,0:T(8,128)} %bitcast.13), calls=%async_computation.1 | async-start | bytes 7340032 | tf_op jit(solution)/shard_map/all_to_all | solution.py:489
  73.8 24.2 %collective-permute-start.2 = (f32[2,2,16,512]{3,2,1,0:T(8,128)S(1)}, f32[2,2,16,512]{3,2,1,0:T(8,128)S(1)}, u32[]{:S(2)}, u32[]{:S(2)}) collective-permute-start(f32[2,2,16,512]{3,2,1,0:T(8,128)S(1)} %get-tuple-element.29), channel_id=1, source_target_pairs={{0,2},{1,3},{2,0},{3,1},{4,6},{5,7},{6,4},{7,5},{8,10},{9,11},{10,... | collective-permute-start | bytes 393224 | tf_op jit(solution)/shard_map/ppermute | solution.py:457
  75.2 22.8 %collective-permute-start.3 = (f32[2,2,16,512]{3,2,1,0:T(8,128)S(1)}, f32[2,2,16,512]{3,2,1,0:T(8,128)S(1)}, u32[]{:S(2)}, u32[]{:S(2)}) collective-permute-start(f32[2,2,16,512]{3,2,1,0:T(8,128)S(1)} %get-tuple-element.30), channel_id=1, source_target_pairs={{0,4},{1,5},{2,6},{3,7},{4,0},{5,1},{6,2},{7,3},{8,12},{9,13},{10,... | collective-permute-start | bytes 393224 | tf_op jit(solution)/shard_map/ppermute | solution.py:457
  77.6 20.8 %collective-permute-start.4 = (f32[2,2,16,512]{3,2,1,0:T(8,128)S(1)}, f32[2,2,16,512]{3,2,1,0:T(8,128)S(1)}, u32[]{:S(2)}, u32[]{:S(2)}) collective-permute-start(f32[2,2,16,512]{3,2,1,0:T(8,128)S(1)} %get-tuple-element.31), channel_id=1, source_target_pairs={{0,6},{1,7},{2,4},{3,5},{4,2},{5,3},{6,0},{7,1},{8,14},{9,15},{10,... | collective-permute-start | bytes 393224 | tf_op jit(solution)/shard_map/ppermute | solution.py:457
  98.5 11.4 %collective-permute-start.5 = (f32[4,2,16,512]{3,2,1,0:T(8,128)S(1)}, f32[4,2,16,512]{3,2,1,0:T(8,128)S(1)}, u32[]{:S(2)}, u32[]{:S(2)}) collective-permute-start(f32[4,2,16,512]{3,2,1,0:T(8,128)S(1)} %pad_maximum_fusion), channel_id=1, source_target_pairs={{0,1},{1,0},{2,3},{3,2},{4,5},{5,4},{6,7},{7,6},{8,9},{9,8},{10,11... | collective-permute-start | bytes 786440 | tf_op jit(solution)/shard_map/ppermute | solution.py:457
  99.3 20.3 %all-to-all-start.2 = ((f32[128,1,128]{2,1,0:T(1,128)}), f32[128,1,128]{2,1,0:T(1,128)S(1)}, u32[]{:S(2)}, u32[]{:S(2)}) async-start(f32[128,1,128]{2,1,0:T(1,128)} %sums.1), calls=%async_computation.2 | async-start | bytes 131072 | tf_op jit(solution)/shard_map/all_to_all | solution.py:497
